TPU v7x, 128 devices: a whole 4x4x4 slice. The times are simulated.
128 devices in a mesh: row: 16 (over z, y), col: 8 (over x, core).
Axes of the slice: x: 4, y: 4, z: 4, core: 2. Of those that a mesh axis runs over, the one named last changes fastest.
Arguments:
- x_blocks: bfloat16 [128, 16, 128, 128], P('row', 'col')
- x_cols: int32 [128, 16], P('row', 'col'), may hold values from 0 to 15, as said below
- x_count: int32 [128, 8], P('row', 'col'), may hold values from 0 to 2, as said below
- y_cols: int32 [128, 96], P('row', 'col'), may hold values from 0 to 15, as said below
- y_count: int32 [128, 8], P('row', 'col'), may hold values from 0 to 12, as said below
- branch_flag: int32 [128], P('row'), may hold values from 0 to 1
Outputs:
- new_blocks: bfloat16 [128, 96, 128, 128], P('row', 'col')
- new_trace: float32 [1], replicated
Inputs may be any that keep to these rules, and one draw needn't show every extreme that they name: `x_cols`: within one block row and one column group, the first x_count slots name distinct block columns; other slots hold arbitrary valid columns. Slot 0 of block row I in group I // 16 names column I % 16. `x_count`: reaches 2; at least 1 for block row I in group I // 16. `y_cols`: within one block row and one column group, the first y_count slots name distinct block columns. Slot 0 of block row I in group I // 16 names column I % 16. `y_count`: reaches 12; at least 1 for block row I in group I // 16.
All inputs are finite; a program needn't handle non-finite values.
Results may differ from a plain program's by a relative error of at most 0.0004.
Values may be sent and summed in bfloat16 or wider, within the bound.
A program may use at most 128 MiB of HBM per device.

v0:
```python
import jax
import jax.numpy as jnp
from jax import lax
from jax.sharding import Mesh
from jax.sharding import PartitionSpec as P

NB = 128
ROWCAP = 2
COL = ("col_0", "col_1")
ROW = ("row_0", "row_1")
ROW_COL = ("row_0", "row_1", "col_0", "col_1")


def in_one_piece(arrays, axis, dim, along):
    both = jnp.concatenate(arrays, axis=along)
    whole, at, outs = (lax.all_gather(both, axis, axis=dim, tiled=True), 0, [])
    for a in arrays:
        outs.append(lax.slice_in_dim(whole, at, at + a.shape[along], axis=along))
        at += a.shape[along]
    return tuple(outs)


def one_axis_at_a_time(shard, axes):
    for axis in axes:
        shard = lax.psum(shard, axis)
    return shard


def pick_blocks(blocks, cols, count, block_keys, wanted, active, offset):
    height = cols.shape[0]
    slot_count = cols.shape[1]
    relative = block_keys - offset
    inside = (relative >= 0) & (relative < height) & active
    clipped = jnp.clip(relative, 0, height - 1).astype(jnp.int32)
    slot_ids = jnp.arange(slot_count, dtype=jnp.int32)
    matched = (
        (cols[clipped] == wanted[..., None])
        & (slot_ids < count[clipped, 0][..., None])
        & inside[..., None]
    )
    found = jnp.any(matched, axis=-1)
    picked = jnp.sum(jnp.where(matched, slot_ids, 0), axis=-1)
    flat_blocks = blocks.reshape((height * slot_count,) + blocks.shape[2:])
    chosen = flat_blocks[clipped * slot_count + picked]
    return jnp.where(found[..., None, None], chosen, jnp.zeros((), blocks.dtype))


def pair_keys(row_cols, row_count, y_cols, y_count, col_width, slot_count):
    pairs = row_cols.shape[1]
    ycap = y_cols.shape[1]
    pair_ids = jnp.arange(pairs, dtype=jnp.int32)
    groups = pair_ids // slot_count
    block_keys = groups[None, :] * col_width + row_cols
    live = (pair_ids % slot_count)[None, :] < jnp.take(row_count, groups, axis=1)
    y_live = jnp.arange(ycap, dtype=jnp.int32)[None, :] < y_count
    shape = (row_cols.shape[0], ycap, pairs)
    block_keys = jnp.broadcast_to(block_keys[:, None, :], shape)
    wanted = jnp.broadcast_to(y_cols[:, :, None], shape)
    active = live[:, None, :] & y_live[:, :, None]
    return (block_keys, wanted, active)


def contract(row_blocks, panel, block_keys, wanted, active, offset):

    def one_row(items):
        row_block, keys, targets, flags = items
        chosen = pick_blocks(panel[0], panel[1], panel[2], keys, targets, flags, offset)
        return jnp.einsum("pab,ypbc->yac", row_block, chosen, preferred_element_type=jnp.float32)

    return lax.map(one_row, (row_blocks, block_keys, wanted, active))


def finish(
    product, own_blocks, own_cols, own_count, y_cols, y_count, branch_flag, row_start, col_start
):
    ycap = y_cols.shape[1]
    y_live = jnp.arange(ycap, dtype=jnp.int32)[None, :] < y_count
    slot_ids = jnp.arange(own_cols.shape[1], dtype=jnp.int32)
    own_match = (own_cols[:, None, :] == y_cols[:, :, None]) & (
        slot_ids[None, None, :] < own_count[:, :, None]
    )
    own_term = jnp.einsum(
        "iyq,iqab->iyab", own_match.astype(jnp.float32), own_blocks.astype(jnp.float32)
    )
    flip = (branch_flag == 1)[:, None, None, None]
    updated = jnp.where(flip, 2.0 * own_term - product, product)
    updated = jnp.where(y_live[..., None, None], updated, jnp.zeros((), updated.dtype))
    rows_global = row_start + jnp.arange(y_cols.shape[0], dtype=jnp.int32)[:, None]
    cols_global = col_start + y_cols
    diagonal = (rows_global == cols_global) & y_live
    traces = jnp.trace(updated, axis1=2, axis2=3)
    trace_part = jnp.sum(jnp.where(diagonal, traces, jnp.zeros((), traces.dtype)))
    return (updated.astype(jnp.bfloat16), trace_part)


def on_device(x_blocks, x_cols, x_count, y_cols, y_count, branch_flag):
    row_blocks, row_cols, row_count = (
        lax.all_gather(x_blocks, COL, axis=1, tiled=True),
        lax.all_gather(x_cols, COL, axis=1, tiled=True),
        lax.all_gather(x_count, COL, axis=1, tiled=True),
    )
    col_width = NB // lax.axis_size(COL)
    block_keys, wanted, active = pair_keys(row_cols, row_count, y_cols, y_count, col_width, ROWCAP)
    panel = (
        lax.all_gather(x_blocks, ROW, axis=0, tiled=True),
        *in_one_piece((x_cols, x_count), ROW, 0, 1),
    )
    product = contract(row_blocks, panel, block_keys, wanted, active, 0)
    row_start = lax.axis_index(ROW) * x_blocks.shape[0]
    col_start = lax.axis_index(COL) * col_width
    updated, trace_part = finish(
        product, x_blocks, x_cols, x_count, y_cols, y_count, branch_flag, row_start, col_start
    )
    total = one_axis_at_a_time(trace_part, ROW_COL)
    return (updated, total.reshape((1,)))


def solution(mesh):
    finer = Mesh(mesh.devices.reshape(4, 4, 4, 2), ("row_0", "row_1", "col_0", "col_1"))
    placed = (P(ROW, COL, None, None), P(ROW, COL), P(ROW, COL), P(ROW, COL), P(ROW, COL), P(ROW))
    return jax.shard_map(
        on_device,
        mesh=finer,
        in_specs=placed,
        out_specs=(P(ROW, COL, None, None), P()),
        check_vma=False,
    )
```

profile of v0, /device:TPU:1, one launch (start us, length us, event | category | flops | bytes accessed | tf_op | source)
XLA Modules:
  0.0 412.5 jit_solution(13879719039861600716)
XLA Ops:
  7.2 0.7 all-gather.8.cloned.1.call-update
  7.9 0.7 all-gather.6.cloned.1.call-update
  8.6 0.7 add_bitcast_fusion.1
  9.4 21.0 %all-gather.1 = s32[16,8,3]{1,2,0:T(4,128)S(1)} all-gather(s32[1,8,3]{1,2,0:T(4,128)S(1)} %add_bitcast_fusion.1), channel_id=1, replica_groups=mesh['row_0'=4,'row_1'=4,'col_0'=4,'col_1'=2] {'row_0','row_1'}, dimensions={0}, use_global_device_ids=true | all-gather | bytes 1632 | tf_op jit(solution)/shard_map/all_gather | solution.py:16
  30.5 0.8 copy.30
  31.2 15.9 %all-gather.2 = s32[8,1,8]{2,1,0:T(1,128)S(1)} all-gather(s32[1,1,8]{2,1,0:T(1,128)} %bitcast.88), channel_id=1, replica_groups=mesh['row_0'=4,'row_1'=4,'col_0'=4,'col_1'=2] {'col_0','col_1'}, dimensions={0}, use_global_device_ids=true | all-gather | bytes 288 | tf_op jit(solution)/shard_map/all_gather | solution.py:100
  47.2 0.6 gather_fusion.3
  48.0 8.4 %all-gather = s32[8,2,8]{2,1,0:T(2,128)S(1)} all-gather(s32[1,2,8]{2,1,0:T(2,128)} %bitcast.87), channel_id=1, replica_groups=mesh['row_0'=4,'row_1'=4,'col_0'=4,'col_1'=2] {'col_0','col_1'}, dimensions={0}, use_global_device_ids=true | all-gather | bytes 576 | tf_op jit(solution)/shard_map/all_gather | solution.py:99
  56.6 0.7 broadcast_compare_fusion
  57.3 0.7 iota_compare_fusion.3
  58.0 0.7 iota_compare_fusion.2
  58.9 59.0 %all-gather.6.cloned.1.call-done = bf16[128,2,128,128]{3,2,1,0:T(8,128)(2,1)} async-done(((bf16[8,2,128,128]{3,2,1,0:T(8,128)(2,1)}), bf16[128,2,128,128]{3,2,1,0:T(8,128)(2,1)}) %all-gather.6.cloned.1.call-update) | async-done | bytes 8388624 | tf_op jit(solution)/shard_map/all_gather | solution.py:105
  117.8 0.8 broadcast_in_dim.103
  118.6 229.1 %while.10 = (s32[]{:T(128)}, f32[8,12,128,128]{2,3,1,0:T(8,128)}, s32[8,12,16]{2,1,0:T(8,128)S(1)}, s32[128,2]{1,0:T(8,128)S(1)}, s32[8,12,16]{2,1,0:T(8,128)S(1...) while((s32[]{:T(128)}, f32[8,12,128,128]{2,3,1,0:T(8,128)}, ...), condition=%wide.region_3.4_spmd, body=%wide.region_0.3_spmd.sunk | while | flops 808459520 | bytes 32805172 | solution.py:70
  118.7 0.7 gather_fusion.1
  119.5 1.5 gather_fusion
  121.9 11.1 %gather_fusion.2 = bf16[192,128,128]{2,1,0:T(8,128)(2,1)} fusion(bf16[256,128,128]{2,1,0:T(8,128)(2,1)} %bitcast.83, s32[1024]{0:T(1024)S(1)} %pad_clamp_fusion.6), kind=kCustom, calls=%fused_computation.2.clone.1 | custom fusion | bytes 12583680 | tf_op jit(solution)/shard_map/while/body/eval_jaxpr/gather | solution.py:44
  133.1 8.6 %copy.49 = bf16[192,128,128]{1,2,0:T(8,128)(2,1)} copy(bf16[192,128,128]{2,1,0:T(8,128)(2,1)} %gather_fusion.2) | data formatting | bytes 12582912 | tf_op jit(solution)/shard_map/while/body/eval_jaxpr/gather | solution.py:44
  141.6 5.6 %fusion.36 = f32[8,12,128,128]{2,3,1,0:T(8,128)} fusion(f32[8,12,128,128]{2,3,1,0:T(8,128)} %get-tuple-element.182, s32[]{:T(128)} %get-tuple-element.181, bf16[12,16,128,128]{2,3,1,0:T(8,128)(2,1)} %bitcast.82, pred[12,16]{1,0:T(8,128)(4,1)S(1)} %get-tuple-element.170, bf16[8,16,128,128]{3,2,1,0:T(8,128)(2,1)} %get-tuple-element.199), kind=kOutput, calls=%fused_computation.9.clone.1 | convolution fusion | flops 808452096 | bytes 7603392 | tf_op jit(solution)/shard_map/while/body/eval_jaxpr/pab,ypbc->yac/dot_general | solution.py:68
  147.3 0.7 gather_fusion.1
  148.1 1.5 gather_fusion
  150.5 11.1 %gather_fusion.2 = bf16[192,128,128]{2,1,0:T(8,128)(2,1)} fusion(bf16[256,128,128]{2,1,0:T(8,128)(2,1)} %bitcast.83, s32[1024]{0:T(1024)S(1)} %pad_clamp_fusion.6), kind=kCustom, calls=%fused_computation.2.clone.1 | custom fusion | bytes 12583680 | tf_op jit(solution)/shard_map/while/body/eval_jaxpr/gather | solution.py:44
  161.7 8.6 %copy.49 = bf16[192,128,128]{1,2,0:T(8,128)(2,1)} copy(bf16[192,128,128]{2,1,0:T(8,128)(2,1)} %gather_fusion.2) | data formatting | bytes 12582912 | tf_op jit(solution)/shard_map/while/body/eval_jaxpr/gather | solution.py:44
  170.3 5.6 %fusion.36 = f32[8,12,128,128]{2,3,1,0:T(8,128)} fusion(f32[8,12,128,128]{2,3,1,0:T(8,128)} %get-tuple-element.182, s32[]{:T(128)} %get-tuple-element.181, bf16[12,16,128,128]{2,3,1,0:T(8,128)(2,1)} %bitcast.82, pred[12,16]{1,0:T(8,128)(4,1)S(1)} %get-tuple-element.170, bf16[8,16,128,128]{3,2,1,0:T(8,128)(2,1)} %get-tuple-element.199), kind=kOutput, calls=%fused_computation.9.clone.1 | convolution fusion | flops 808452096 | bytes 7603392 | tf_op jit(solution)/shard_map/while/body/eval_jaxpr/pab,ypbc->yac/dot_general | solution.py:68
  176.0 0.7 gather_fusion.1
  176.7 1.5 gather_fusion
  178.4 0.4 fusion.35
  179.2 11.1 %gather_fusion.2 = bf16[192,128,128]{2,1,0:T(8,128)(2,1)} fusion(bf16[256,128,128]{2,1,0:T(8,128)(2,1)} %bitcast.83, s32[1024]{0:T(1024)S(1)} %pad_clamp_fusion.6), kind=kCustom, calls=%fused_computation.2.clone.1 | custom fusion | bytes 12583680 | tf_op jit(solution)/shard_map/while/body/eval_jaxpr/gather | solution.py:44
  190.3 8.6 %copy.49 = bf16[192,128,128]{1,2,0:T(8,128)(2,1)} copy(bf16[192,128,128]{2,1,0:T(8,128)(2,1)} %gather_fusion.2) | data formatting | bytes 12582912 | tf_op jit(solution)/shard_map/while/body/eval_jaxpr/gather | solution.py:44
  198.9 5.6 %fusion.36 = f32[8,12,128,128]{2,3,1,0:T(8,128)} fusion(f32[8,12,128,128]{2,3,1,0:T(8,128)} %get-tuple-element.182, s32[]{:T(128)} %get-tuple-element.181, bf16[12,16,128,128]{2,3,1,0:T(8,128)(2,1)} %bitcast.82, pred[12,16]{1,0:T(8,128)(4,1)S(1)} %get-tuple-element.170, bf16[8,16,128,128]{3,2,1,0:T(8,128)(2,1)} %get-tuple-element.199), kind=kOutput, calls=%fused_computation.9.clone.1 | convolution fusion | flops 808452096 | bytes 7603392 | tf_op jit(solution)/shard_map/while/body/eval_jaxpr/pab,ypbc->yac/dot_general | solution.py:68
  204.6 0.7 gather_fusion.1
  205.3 1.5 gather_fusion
  207.0 0.4 fusion.35
  207.8 11.1 %gather_fusion.2 = bf16[192,128,128]{2,1,0:T(8,128)(2,1)} fusion(bf16[256,128,128]{2,1,0:T(8,128)(2,1)} %bitcast.83, s32[1024]{0:T(1024)S(1)} %pad_clamp_fusion.6), kind=kCustom, calls=%fused_computation.2.clone.1 | custom fusion | bytes 12583680 | tf_op jit(solution)/shard_map/while/body/eval_jaxpr/gather | solution.py:44
  218.9 8.6 %copy.49 = bf16[192,128,128]{1,2,0:T(8,128)(2,1)} copy(bf16[192,128,128]{2,1,0:T(8,128)(2,1)} %gather_fusion.2) | data formatting | bytes 12582912 | tf_op jit(solution)/shard_map/while/body/eval_jaxpr/gather | solution.py:44
  227.5 5.6 %fusion.36 = f32[8,12,128,128]{2,3,1,0:T(8,128)} fusion(f32[8,12,128,128]{2,3,1,0:T(8,128)} %get-tuple-element.182, s32[]{:T(128)} %get-tuple-element.181, bf16[12,16,128,128]{2,3,1,0:T(8,128)(2,1)} %bitcast.82, pred[12,16]{1,0:T(8,128)(4,1)S(1)} %get-tuple-element.170, bf16[8,16,128,128]{3,2,1,0:T(8,128)(2,1)} %get-tuple-element.199), kind=kOutput, calls=%fused_computation.9.clone.1 | convolution fusion | flops 808452096 | bytes 7603392 | tf_op jit(solution)/shard_map/while/body/eval_jaxpr/pab,ypbc->yac/dot_general | solution.py:68
  233.2 0.7 gather_fusion.1
  234.0 1.5 gather_fusion
  236.4 11.1 %gather_fusion.2 = bf16[192,128,128]{2,1,0:T(8,128)(2,1)} fusion(bf16[256,128,128]{2,1,0:T(8,128)(2,1)} %bitcast.83, s32[1024]{0:T(1024)S(1)} %pad_clamp_fusion.6), kind=kCustom, calls=%fused_computation.2.clone.1 | custom fusion | bytes 12583680 | tf_op jit(solution)/shard_map/while/body/eval_jaxpr/gather | solution.py:44
  247.6 8.6 %copy.49 = bf16[192,128,128]{1,2,0:T(8,128)(2,1)} copy(bf16[192,128,128]{2,1,0:T(8,128)(2,1)} %gather_fusion.2) | data formatting | bytes 12582912 | tf_op jit(solution)/shard_map/while/body/eval_jaxpr/gather | solution.py:44
  256.1 5.6 %fusion.36 = f32[8,12,128,128]{2,3,1,0:T(8,128)} fusion(f32[8,12,128,128]{2,3,1,0:T(8,128)} %get-tuple-element.182, s32[]{:T(128)} %get-tuple-element.181, bf16[12,16,128,128]{2,3,1,0:T(8,128)(2,1)} %bitcast.82, pred[12,16]{1,0:T(8,128)(4,1)S(1)} %get-tuple-element.170, bf16[8,16,128,128]{3,2,1,0:T(8,128)(2,1)} %get-tuple-element.199), kind=kOutput, calls=%fused_computation.9.clone.1 | convolution fusion | flops 808452096 | bytes 7603392 | tf_op jit(solution)/shard_map/while/body/eval_jaxpr/pab,ypbc->yac/dot_general | solution.py:68
  261.8 0.7 gather_fusion.1
  262.6 1.5 gather_fusion
  265.0 11.2 %gather_fusion.2 = bf16[192,128,128]{2,1,0:T(8,128)(2,1)} fusion(bf16[256,128,128]{2,1,0:T(8,128)(2,1)} %bitcast.83, s32[1024]{0:T(1024)S(1)} %pad_clamp_fusion.6), kind=kCustom, calls=%fused_computation.2.clone.1 | custom fusion | bytes 12583680 | tf_op jit(solution)/shard_map/while/body/eval_jaxpr/gather | solution.py:44
  276.2 8.6 %copy.49 = bf16[192,128,128]{1,2,0:T(8,128)(2,1)} copy(bf16[192,128,128]{2,1,0:T(8,128)(2,1)} %gather_fusion.2) | data formatting | bytes 12582912 | tf_op jit(solution)/shard_map/while/body/eval_jaxpr/gather | solution.py:44
  284.8 5.6 %fusion.36 = f32[8,12,128,128]{2,3,1,0:T(8,128)} fusion(f32[8,12,128,128]{2,3,1,0:T(8,128)} %get-tuple-element.182, s32[]{:T(128)} %get-tuple-element.181, bf16[12,16,128,128]{2,3,1,0:T(8,128)(2,1)} %bitcast.82, pred[12,16]{1,0:T(8,128)(4,1)S(1)} %get-tuple-element.170, bf16[8,16,128,128]{3,2,1,0:T(8,128)(2,1)} %get-tuple-element.199), kind=kOutput, calls=%fused_computation.9.clone.1 | convolution fusion | flops 808452096 | bytes 7603392 | tf_op jit(solution)/shard_map/while/body/eval_jaxpr/pab,ypbc->yac/dot_general | solution.py:68
  290.5 0.7 gather_fusion.1
  291.3 1.5 gather_fusion
  293.7 11.1 %gather_fusion.2 = bf16[192,128,128]{2,1,0:T(8,128)(2,1)} fusion(bf16[256,128,128]{2,1,0:T(8,128)(2,1)} %bitcast.83, s32[1024]{0:T(1024)S(1)} %pad_clamp_fusion.6), kind=kCustom, calls=%fused_computation.2.clone.1 | custom fusion | bytes 12583680 | tf_op jit(solution)/shard_map/while/body/eval_jaxpr/gather | solution.py:44
  304.9 8.6 %copy.49 = bf16[192,128,128]{1,2,0:T(8,128)(2,1)} copy(bf16[192,128,128]{2,1,0:T(8,128)(2,1)} %gather_fusion.2) | data formatting | bytes 12582912 | tf_op jit(solution)/shard_map/while/body/eval_jaxpr/gather | solution.py:44
  313.4 5.7 %fusion.36 = f32[8,12,128,128]{2,3,1,0:T(8,128)} fusion(f32[8,12,128,128]{2,3,1,0:T(8,128)} %get-tuple-element.182, s32[]{:T(128)} %get-tuple-element.181, bf16[12,16,128,128]{2,3,1,0:T(8,128)(2,1)} %bitcast.82, pred[12,16]{1,0:T(8,128)(4,1)S(1)} %get-tuple-element.170, bf16[8,16,128,128]{3,2,1,0:T(8,128)(2,1)} %get-tuple-element.199), kind=kOutput, calls=%fused_computation.9.clone.1 | convolution fusion | flops 808452096 | bytes 7603392 | tf_op jit(solution)/shard_map/while/body/eval_jaxpr/pab,ypbc->yac/dot_general | solution.py:68
  319.2 0.7 gather_fusion.1
  320.0 1.5 gather_fusion
  322.4 11.1 %gather_fusion.2 = bf16[192,128,128]{2,1,0:T(8,128)(2,1)} fusion(bf16[256,128,128]{2,1,0:T(8,128)(2,1)} %bitcast.83, s32[1024]{0:T(1024)S(1)} %pad_clamp_fusion.6), kind=kCustom, calls=%fused_computation.2.clone.1 | custom fusion | bytes 12583680 | tf_op jit(solution)/shard_map/while/body/eval_jaxpr/gather | solution.py:44
  333.6 8.6 %copy.49 = bf16[192,128,128]{1,2,0:T(8,128)(2,1)} copy(bf16[192,128,128]{2,1,0:T(8,128)(2,1)} %gather_fusion.2) | data formatting | bytes 12582912 | tf_op jit(solution)/shard_map/while/body/eval_jaxpr/gather | solution.py:44
  342.1 5.6 %fusion.36 = f32[8,12,128,128]{2,3,1,0:T(8,128)} fusion(f32[8,12,128,128]{2,3,1,0:T(8,128)} %get-tuple-element.182, s32[]{:T(128)} %get-tuple-element.181, bf16[12,16,128,128]{2,3,1,0:T(8,128)(2,1)} %bitcast.82, pred[12,16]{1,0:T(8,128)(4,1)S(1)} %get-tuple-element.170, bf16[8,16,128,128]{3,2,1,0:T(8,128)(2,1)} %get-tuple-element.199), kind=kOutput, calls=%fused_computation.9.clone.1 | convolution fusion | flops 808452096 | bytes 7603392 | tf_op jit(solution)/shard_map/while/body/eval_jaxpr/pab,ypbc->yac/dot_general | solution.py:68
  347.7 9.1 %copy.37 = f32[8,12,128,128]{3,1,2,0:T(8,128)} copy(f32[8,12,128,128]{2,3,1,0:T(8,128)} %get-tuple-element.49) | data formatting | bytes 12582912 | tf_op jit(solution)/shard_map/while | solution.py:70
  356.8 8.6 %select_reduce_fusion.1 = (f32[8,12]{1,0:T(8,128)S(1)}, bf16[8,12,128,128]{3,1,2,0:T(8,128)(2,1)}) fusion(pred[128,128]{1,0:T(8,128)(4,1)S(1)} %iota_compare_fusion.1, f32[8,12,128,128]{3,1,2,0:T(8,128)} %copy.37, bf16[8,2,128,128]{3,2,1,0:T(8,128)(2,1)S(1)} %copy-done, pred[8,2]{1,0:T(8,128)(4,1)S(1)} %iota_compare_fusion.2, s32[8,12]{1,0:T(8,128)S(1)} %copy-done.1, ...), kind=kOutput, calls=%fused_computation.29 | convolution fusion | flops 17301792 | bytes 9978808 | tf_op jit(solution)/shard_map/iyq,iqab->iyab/dot_general | solution.py:82
  365.4 0.7 select_reduce_fusion.2
  366.1 9.1 %psum.28 = f32[]{:T(128)} all-reduce(f32[]{:T(128)} %select_reduce_fusion.2), channel_id=1, replica_groups=mesh['row_0'=4,'row_1'=4,'col_0'=4,'col_1'=2] {'row_0'}, use_global_device_ids=true, to_apply=%region_6.7 | all-reduce | flops 1 | bytes 8 | tf_op jit(solution)/shard_map/psum | solution.py:25
  375.1 7.2 %psum.29 = f32[]{:T(128)} all-reduce(f32[]{:T(128)} %psum.28), channel_id=1, replica_groups=mesh['row_0'=4,'row_1'=4,'col_0'=4,'col_1'=2] {'row_1'}, use_global_device_ids=true, to_apply=%region_7.8 | all-reduce | flops 1 | bytes 8 | tf_op jit(solution)/shard_map/psum | solution.py:25
  382.3 9.0 %psum.30 = f32[]{:T(128)} all-reduce(f32[]{:T(128)} %psum.29), channel_id=1, replica_groups=mesh['row_0'=4,'row_1'=4,'col_0'=4,'col_1'=2] {'col_0'}, use_global_device_ids=true, to_apply=%region_8.9 | all-reduce | flops 1 | bytes 8 | tf_op jit(solution)/shard_map/psum | solution.py:25
  391.3 9.6 %psum.31 = f32[1]{0:T(128)} all-reduce(f32[1]{0:T(128)} %bitcast.27), channel_id=1, replica_groups=mesh['row_0'=4,'row_1'=4,'col_0'=4,'col_1'=2] {'col_1'}, use_global_device_ids=true, to_apply=%region_9.10 | all-reduce | flops 1 | bytes 8 | tf_op jit(solution)/shard_map/psum | solution.py:25
  400.9 4.7 %copy.39 = bf16[8,12,128,128]{3,2,1,0:T(8,128)(2,1)} copy(bf16[8,12,128,128]{3,1,2,0:T(8,128)(2,1)} %get-tuple-element.106) | data formatting | bytes 6291456
  (122 shorter events, 8.4 us)
Async XLA Ops:
  7.2 51.7 %all-gather.8.cloned.1.call-start = ((), (), s32[]{:S(2)}) async-start(), calls=%async_computation.1 | async-start | bytes 4718592 | tf_op jit(solution)/shard_map/all_gather | solution.py:98
  7.9 109.9 %all-gather.6.cloned.1.call-start = ((), (), s32[]{:S(2)}) async-start(), calls=%async_computation | async-start | bytes 8912896 | tf_op jit(solution)/shard_map/all_gather | solution.py:105
  347.7 9.1 %copy-start = (bf16[8,2,128,128]{3,2,1,0:T(8,128)(2,1)S(1)}, bf16[8,2,128,128]{3,2,1,0:T(8,128)(2,1)}, u32[]{:S(2)}) copy-start(bf16[8,2,128,128]{3,2,1,0:T(8,128)(2,1)} %param.8) | copy-start | bytes 1572868
  347.7 9.1 %copy-start.1 = (s32[8,12]{1,0:T(8,128)S(1)}, s32[8,12]{1,0:T(8,128)}, u32[]{:S(2)}) copy-start(s32[8,12]{1,0:T(8,128)} %param.11) | copy-start | bytes 1156
  356.8 8.6 %copy-start.2 = (s32[8,1]{0,1:T(1,128)S(1)}, s32[8,1]{0,1:T(1,128)}, u32[]{:S(2)}) copy-start(s32[8,1]{0,1:T(1,128)} %param.12) | copy-start | bytes 100
Sparse Core Ops, SparseCore 0:
  9.7 35.6 all-gather.7
  47.5 70.3 all-gather.5
where the time goes:
time: 415 us; the launch traced here: 412 us
  local copies, waits for them, and re-layouts  194 us (47%)
  blocking collectives  80.1 us (19%)
  waiting for transfers between devices  60.4 us (15%)
  matrix products  53.4 us (13%)
  between operations  14.1 us (3%)
  other arithmetic  9.6 us (2%)
    gather x16, local copies, waits for them, and re-layouts, pick_blocks(): chosen = flat_blocks[clipped * slot_count + picked]  158 us
    all_gather x1, waiting for transfers between devices, on_device(): lax.all_gather(x_blocks, ROW, axis=0, tiled=True)  59 us
    dot_general x8, matrix products, one_row(): jnp.einsum('pab,ypbc->yac', row_block, chosen, preferred_element_type=jnp...  44.8 us
    psum x4, blocking collectives, one_axis_at_a_time(): shard = lax.psum(shard, axis)  34.8 us
    all_gather x1, blocking collectives, in_one_piece(): whole, at, outs = (lax.all_gather(both, axis, axis=dim, tiled=True), 0, [])  21 us
    all_gather x1, blocking collectives, on_device(): lax.all_gather(x_count, COL, axis=1, tiled=True)  15.9 us
    gather x16, local copies, waits for them, and re-layouts, pick_blocks(): count[clipped, 0][..., None]  13 us
    while x2, local copies, waits for them, and re-layouts, contract(): return lax.map(one_row, (row_blocks, block_keys, wanted, active))  9.22 us
  transfers between devices with their start and end apart: 2, of which 1 were waited for; matrix products, arithmetic and copies ran while one was open for 1% of the time, Pallas kernels for 0%

commit v1 on v0

v1 whole, which is shorter than its diff:
```python
import jax
import jax.numpy as jnp
from jax import lax
from jax.experimental import pallas as pl
from jax.experimental.pallas import tpu as pltpu
from jax.sharding import Mesh
from jax.sharding import PartitionSpec as P

BS = 128
ROWS = 8
CAP = 2
YCAP = 12
OWN = ROWS * CAP
LINE = ("z", "y")
ALL = ("z", "y", "x", "core")
MESH_ID = pl.DeviceIdType.MESH
ZERO = 256


def gather_kernel(x_ref, m_ref, strip, panel, smeta, pmeta, psend, precv, xsend, xrecv, csend, crecv, lsem):
    place = {a: lax.axis_index(a) for a in ("z", "y", "x")}
    after = {a: lax.rem(v + 1, 4) for a, v in place.items()}
    before = {a: lax.rem(v + 3, 4) for a, v in place.items()}
    across = {a: lax.rem(v + 2, 4) for a, v in place.items()}
    core = lax.axis_index("core")
    z, y, x = place["z"], place["y"], place["x"]

    barrier = pltpu.get_barrier_semaphore()
    peers = [{a: to[a]} for a in ("z", "y", "x") for to in (after, before)] + [{"core": 1 - core}]
    for peer in peers:
        pl.semaphore_signal(barrier, inc=1, device_id=peer, device_id_type=MESH_ID)

    here = z * 4 + y
    local = [
        pltpu.make_async_copy(x_ref, panel.at[here], lsem.at[0]),
        pltpu.make_async_copy(x_ref, strip.at[x * 2 + core], lsem.at[1]),
        pltpu.make_async_copy(m_ref, pmeta.at[here], lsem.at[2]),
        pltpu.make_async_copy(m_ref, smeta.at[x * 2 + core], lsem.at[3]),
    ]
    for c in local:
        c.start()
    panel[16, 0] = jnp.zeros((BS, BS), jnp.bfloat16)
    pl.semaphore_wait(barrier, len(peers))

    sends = []

    def copy(src, dst, ss, rs, peer):
        return pltpu.make_async_remote_copy(
            src_ref=src, dst_ref=dst, send_sem=ss, recv_sem=rs, device_id=peer, device_id_type=MESH_ID
        )

    def start(*args):
        c = copy(*args)
        c.start()
        sends.append(c)

    class Ring:
        def __init__(self, axis, at, ssem, rsem, j, halves=2):
            self.axis, self.at, self.ssem, self.rsem, self.j, self.halves = axis, at, ssem, rsem, j, halves

        def own(self, src=None):
            dst = self.at(place[self.axis], None)
            src = dst if src is None else src
            for q, to in ((0, after), (1, before)):
                start(src, dst, self.ssem.at[self.j, q], self.rsem.at[self.j, q], {self.axis: to[self.axis]})

        def arrive(self, q):
            owner = (before, after)[q][self.axis]
            dst = self.at(owner, None)
            copy(dst, dst, self.ssem.at[self.j, q], self.rsem.at[self.j, q], {self.axis: owner}).wait_recv()
            if q < self.halves:
                half = self.at(owner, q if self.halves == 2 else None)
                to = (after, before)[q][self.axis]
                start(half, half, self.ssem.at[self.j, 2 + q], self.rsem.at[self.j, 2 + q], {self.axis: to})

        def arrive_across(self):
            for q in range(self.halves):
                half = self.at(across[self.axis], q if self.halves == 2 else None)
                copy(half, half, self.ssem.at[self.j, 2 + q], self.rsem.at[self.j, 2 + q],
                     {self.axis: before[self.axis]}).wait_recv()

    def panel_ring(axis, d, lo, j):
        def at(p, half):
            o = lax.rem((y if axis == "z" else z) + d, 4)
            g = p * 4 + o if axis == "z" else o * 4 + p
            return panel.at[g, pl.ds(lo, 8)] if half is None else panel.at[g, pl.ds(lo + 4 * half, 4)]

        return Ring(axis, at, psend, precv, j)

    def pmeta_ring(axis, d, j):
        def at(p, half):
            o = lax.rem((y if axis == "z" else z) + d, 4)
            return pmeta.at[p * 4 + o if axis == "z" else o * 4 + p]

        return Ring(axis, at, psend, precv, j, halves=1)

    def strip_at(p, half):
        g = p * 2 + core
        return strip.at[g] if half is None else strip.at[g, pl.ds(8 * half, 8)]

    az, by = panel_ring("z", 0, 0, 0), panel_ring("y", 0, 8, 1)
    ay = {d: panel_ring("y", d, 0, j) for d, j in ((0, 2), (3, 4), (1, 5), (2, 8))}
    bz = {d: panel_ring("z", d, 8, j) for d, j in ((0, 3), (3, 6), (1, 7), (2, 9))}
    mz = pmeta_ring("z", 0, 10)
    my = {d: pmeta_ring("y", d, j) for d, j in ((0, 11), (3, 12), (1, 13), (2, 14))}
    xs = Ring("x", strip_at, xsend, xrecv, 0)
    xm = Ring("x", lambda p, half: smeta.at[p * 2 + core], xsend, xrecv, 1, halves=1)

    def swap(p, j):
        g = p * 2 + core
        start(strip.at[g], strip.at[g], csend.at[0, j], crecv.at[0, j], {"core": 1 - core})
        start(smeta.at[g], smeta.at[g], csend.at[1, j], crecv.at[1, j], {"core": 1 - core})

    az.own(x_ref.at[pl.ds(0, 8)])
    by.own(x_ref.at[pl.ds(8, 8)])
    mz.own(m_ref)
    my[0].own(m_ref)
    ay[0].own(x_ref.at[pl.ds(0, 8)])
    bz[0].own(x_ref.at[pl.ds(8, 8)])
    xm.own(m_ref)
    xs.own(x_ref)
    for c in local:
        c.wait()
    swap(x, 0)
    for q, d in ((0, 3), (1, 1)):
        az.arrive(q)
        ay[d].own()
        by.arrive(q)
        bz[d].own()
        mz.arrive(q)
        my[d].own()
        my[0].arrive(q)
    for q in (0, 1):
        xs.arrive(q)
        xm.arrive(q)
        swap((before, after)[q]["x"], 1 + q)
    for q in (0, 1):
        ay[0].arrive(q)
        bz[0].arrive(q)
    az.arrive_across()
    ay[2].own()
    by.arrive_across()
    bz[2].own()
    mz.arrive_across()
    my[2].own()
    my[0].arrive_across()
    for d in (3, 1):
        for q in (0, 1):
            ay[d].arrive(q)
            bz[d].arrive(q)
            my[d].arrive(q)
    xs.arrive_across()
    xm.arrive_across()
    swap(across["x"], 3)
    for q in (0, 1):
        ay[2].arrive(q)
        bz[2].arrive(q)
        my[2].arrive(q)
    for d in (0, 3, 1, 2):
        ay[d].arrive_across()
        bz[d].arrive_across()
        if d:
            my[d].arrive_across()
    for p, j in ((x, 0), (before["x"], 1), (after["x"], 2), (across["x"], 3)):
        g = p * 2 + 1 - core
        copy(strip.at[g], strip.at[g], csend.at[0, j], crecv.at[0, j], {"core": 1 - core}).wait_recv()
        copy(smeta.at[g], smeta.at[g], csend.at[1, j], crecv.at[1, j], {"core": 1 - core}).wait_recv()
    for c in sends:
        c.wait_send()


def product_kernel(where, smeta, pmeta, y_cols, y_count, flag, strip, panel, out, part, obuf, diag,
                   slot, cnt, la, lb, own, osem):
    chunk, on_diag = where[0], where[1]
    diag[...] = jnp.zeros_like(diag)

    def row(i, carry):
        live_y = y_count[i, 0]
        for j in range(17):
            slot[j] = YCAP
        for t in range(YCAP):
            slot[jnp.where(t < live_y, y_cols[i, t], 16)] = t
        slot[16] = YCAP
        for t in range(YCAP + 1):
            cnt[t] = 0
            own[t] = ZERO
            la[t, 0] = 0
            la[t, 1] = 0
            lb[t, 0] = ZERO
            lb[t, 1] = ZERO
        for q in range(CAP):
            live = q < pmeta[chunk, 0, i * 4 + 2]
            t = slot[jnp.where(live, pmeta[chunk, 0, i * 4 + q], 16)]
            own[t] = chunk * OWN + i * CAP + q

        def pairs(g, c):
            n_live = smeta[g, 0, i * 4 + 2]
            for s in range(CAP):
                @pl.when(s < n_live)
                def _():
                    k = g * 16 + smeta[g, 0, i * 4 + s]
                    kc, kr = k // 8, k % 8
                    n_in = pmeta[kc, 0, kr * 4 + 2]
                    for w in range(CAP):
                        t = slot[jnp.where(w < n_in, pmeta[kc, 0, kr * 4 + w], 16)]
                        n = cnt[t]
                        la[t, n] = g * OWN + i * CAP + s
                        lb[t, n] = k * CAP + w
                        cnt[t] = n + 1
            return c

        lax.fori_loop(0, 8, pairs, 0)
        flip = flag[i] == 1
        sign = jnp.where(flip, -1.0, 1.0)
        twice = jnp.where(flip, 2.0, 0.0)

        def dot2(t, n):
            a = jnp.concatenate([strip[la[t, n]], strip[la[t, n + 1]]], axis=1)
            b = jnp.concatenate([panel[lb[t, n]], panel[lb[t, n + 1]]], axis=0)
            return jnp.dot(a, b, preferred_element_type=jnp.float32)

        def finish(t, product):
            return sign * product + twice * panel[own[t]].astype(jnp.float32)

        for t in range(YCAP):
            updated = finish(t, dot2(t, 0))
            obuf[i, t] = updated.astype(jnp.bfloat16)
            if t == 0:
                diag[1] = updated

        def more(t, c):
            n = cnt[t]

            @pl.when(n > 2)
            def _():
                la[t, n] = 0
                lb[t, n] = ZERO
                product = lax.fori_loop(
                    1, (n + 1) // 2, lambda h, acc: acc + dot2(t, h * 2), dot2(t, 0)
                )
                updated = finish(t, product)
                obuf[i, t] = updated.astype(jnp.bfloat16)

                @pl.when(t == 0)
                def _():
                    diag[1] = updated

            return c

        lax.fori_loop(0, YCAP, more, 0)
        diag[0] += diag[1]
        pltpu.make_async_copy(obuf.at[i], out.at[i], osem.at[i]).start()
        return carry

    lax.fori_loop(0, ROWS, row, 0)
    eye = lax.broadcasted_iota(jnp.int32, (BS, BS), 0) == lax.broadcasted_iota(jnp.int32, (BS, BS), 1)
    total = jnp.sum(jnp.where(eye & (on_diag == 1), diag[0], 0.0))
    part[...] = jnp.full(part.shape, total)
    for i in range(ROWS):
        pltpu.make_async_copy(obuf.at[i], out.at[i], osem.at[i]).wait()


def on_device(x_blocks, x_cols, x_count, y_cols, y_count, branch_flag):
    meta = jnp.concatenate([x_cols, x_count, branch_flag[:, None]], axis=1)
    meta = jnp.pad(meta.reshape(1, 32), ((0, 0), (0, 96)))
    vmem, anywhere, smem = (pl.BlockSpec(memory_space=m) for m in (pltpu.VMEM, pl.ANY, pltpu.SMEM))
    blocks = x_blocks.reshape(OWN, BS, BS)
    dma = pltpu.SemaphoreType.DMA
    strip, panel, smeta, pmeta = pl.pallas_call(
        gather_kernel,
        out_shape=[
            pltpu.VMEM((8, OWN, BS, BS), jnp.bfloat16),
            pltpu.VMEM((17, OWN, BS, BS), jnp.bfloat16),
            pltpu.VMEM((8, 1, BS), jnp.int32),
            pltpu.VMEM((16, 1, BS), jnp.int32),
        ],
        in_specs=[anywhere, vmem],
        out_specs=[vmem] * 4,
        scratch_shapes=[dma((15, 4)), dma((15, 4)), dma((2, 4)), dma((2, 4)), dma((2, 4)), dma((2, 4)), dma((4,))],
        compiler_params=pltpu.CompilerParams(
            collective_id=0, has_side_effects=True, vmem_limit_bytes=16 << 20
        ),
    )(blocks, meta)
    chunk = lax.axis_index("z") * 4 + lax.axis_index("y")
    group = lax.axis_index("x") * 2 + lax.axis_index("core")
    where = jnp.stack([chunk, (chunk // 2 == group).astype(jnp.int32)])
    out, part = pl.pallas_call(
        product_kernel,
        out_shape=[
            jax.ShapeDtypeStruct((ROWS, YCAP, BS, BS), jnp.bfloat16),
            jax.ShapeDtypeStruct((8, BS), jnp.float32),
        ],
        in_specs=[smem] * 6 + [vmem] * 2,
        out_specs=[anywhere, vmem],
        scratch_shapes=[
            pltpu.VMEM((ROWS, YCAP, BS, BS), jnp.bfloat16),
            pltpu.VMEM((2, BS, BS), jnp.float32),
            pltpu.SMEM((17,), jnp.int32),
            pltpu.SMEM((YCAP + 1,), jnp.int32),
            pltpu.SMEM((YCAP + 1, 40), jnp.int32),
            pltpu.SMEM((YCAP + 1, 40), jnp.int32),
            pltpu.SMEM((YCAP + 1,), jnp.int32),
            dma((ROWS,)),
        ],
        compiler_params=pltpu.CompilerParams(vmem_limit_bytes=16 << 20),
    )(where, smeta, pmeta, y_cols, y_count, branch_flag,
      strip.reshape(8 * OWN, BS, BS), panel.reshape(17 * OWN, BS, BS))
    total = lax.psum(part[0, 0], ALL)
    return out, total.reshape((1,))


def solution(mesh):
    finer = Mesh(mesh.devices.reshape(4, 4, 4, 2), ALL)
    placed = (
        P(LINE, ("x", "core"), None, None),
        P(LINE, ("x", "core")),
        P(LINE, ("x", "core")),
        P(LINE, ("x", "core")),
        P(LINE, ("x", "core")),
        P(LINE),
    )
    return jax.shard_map(
        on_device,
        mesh=finer,
        in_specs=placed,
        out_specs=(P(LINE, ("x", "core"), None, None), P()),
        check_vma=False,
    )
```

time: 415 us -> 134 us (0.32)
  local copies, waits for them, and re-layouts: 194 us -> 3.8 us
  Pallas kernels: 0 us -> 62.6 us
  waiting for transfers between devices: 60.4 us -> 0 us
  matrix products: 53.4 us -> 0 us
  blocking collectives: 80.1 us -> 65.9 us
  between operations: 14.1 us -> 0.68 us
  other arithmetic: 9.6 us -> 0.8 us
    gather x41 -> x0, local copies, waits for them, and re-layouts: 177 us -> none  [the longest x16 158 us: pick_blocks(): chosen = flat_blocks[clipped * slot_count + picked]]
    pallas_call x0 -> x2, Pallas kernels: none -> 62.6 us  [the longest x1 51.2 us: on_device(): pl.pallas_call(gather_kernel, out_shape=[pltpu.VMEM((8, OWN, BS, BS), jnp...]
    all_gather x2 -> x0, waiting for transfers between devices: 59 us -> none  [the longest x1 59 us: on_device(): lax.all_gather(x_blocks, ROW, axis=0, tiled=True)]
    dot_general x9 -> x0, matrix products: 53.4 us -> none  [the longest x8 44.8 us: one_row(): jnp.einsum('pab,ypbc->yac', row_block, chosen, preferred_element_type=jnp...]
    all_gather x3 -> x0, blocking collectives: 45.3 us -> none  [the longest x1 21 us: in_one_piece(): whole, at, outs = (lax.all_gather(both, axis, axis=dim, tiled=True), 0, [])]
    psum x4 -> x1, blocking collectives: 34.8 us -> 65.9 us  [on_device(): total = lax.psum(part[0, 0], ALL)]
    while x2 -> x0, local copies, waits for them, and re-layouts: 9.22 us -> none  [contract(): return lax.map(one_row, (row_blocks, block_keys, wanted, active))]
  transfers between devices with their start and end apart: 2 -> 0, of which waited for: 1 -> 0; matrix products, arithmetic and copies ran while one was open for 1% -> 0% of each run, Pallas kernels for 0% -> 0%
where the time goes in v1:
time: 134 us
  blocking collectives  65.9 us (49%)
  Pallas kernels  62.6 us (47%)
  local copies, waits for them, and re-layouts  3.8 us (3%)
    psum x1, blocking collectives, on_device(): total = lax.psum(part[0, 0], ALL)  65.9 us
    pallas_call x1, Pallas kernels, on_device(): pl.pallas_call(gather_kernel, out_shape=[pltpu.VMEM((8, OWN, BS, BS), jnp...  51.2 us
    pallas_call x1, Pallas kernels, on_device(): pl.pallas_call(product_kernel, out_shape=[jax.ShapeDtypeStruct((ROWS, YCA...  11.5 us
    unnamed x7, local copies, waits for them, and re-layouts  3.11 us

profile of v1, /device:TPU:1, one launch (start us, length us, event | category | flops | bytes accessed | tf_op | source)
XLA Modules:
  0.0 133.8 jit_solution(13977739635579901831)
XLA Ops:
  0.6 0.1 pad_add_fusion.1.where
  0.7 0.7 pad_add_fusion
  1.4 0.1 copy.10
  1.5 0.1 reshape.20
  1.6 0.7 copy.11.y_count
  2.4 0.0 copy-start
  2.4 1.0 copy-done
  3.4 51.2 %shard_map.77 = (bf16[8,16,128,128]{3,2,1,0:T(8,128)(2,1)S(1)}, bf16[17,16,128,128]{3,2,1,0:T(8,128)(2,1)S(1)}, s32[8,1,128]{2,1,0:T(1,128)S(1)}, s32[16,1,128]{2,1,0:T(1,128)S(1)}) custom-call(bf16[16,128,128]{2,1,0:T(8,128)(2,1)S(1)} %bitcast.9, s32[1,128]{1,0:T(1,128)S(1)} %pad.4.m_ref), custom_call_target="tpu_custom_call" | custom-call | tf_op jit(solution)/shard_map/pallas_call | solution.py:269
  54.6 0.0 copy-start.1
  54.6 0.7 copy-done.1
  55.2 0.0 copy-start.2
  55.2 0.7 copy-done.2
  55.9 11.5 %shard_map.78 = (bf16[8,12,128,128]{3,2,1,0:T(8,128)(2,1)}, f32[8,128]{1,0:T(8,128)S(1)}) custom-call(s32[2]{0:T(128)S(1)} %pad_add_fusion.1.where, s32[8,1,128]{2,1,0:T(1,128)S(1)} %get-tuple-element.8.smeta, s32[16,1,128]{2,1,0:T(1,128)S(1)} %get-tuple-element.9.pmeta, s32[8,12]{1,0:T(8,128)S(1)} %copy-done.1, s32[8,1]{1,0:T(8,128)S(1)} %copy.11.y_count, ...), custom_call_target="tpu_custom_call" | custom-call | tf_op jit(solution)/shard_map/pallas_call | solution.py:287
  67.4 0.5 slice.3
  67.9 65.9 %psum.7 = f32[1]{0:T(128)} all-reduce(f32[1]{0:T(128)} %bitcast.6), channel_id=1, replica_groups=mesh['z'=4,'y'=4,'x'=4,'core'=2] {'z','y','x','core'}, use_global_device_ids=true, to_apply=%region_0.1 | all-reduce | flops 1 | bytes 8 | tf_op jit(solution)/shard_map/psum | solution.py:308
  (1 shorter events, 0.0 us)
Async XLA Ops:
  2.4 1.0 copy-start
  54.6 0.7 copy-start.1
  55.2 0.7 copy-start.2

commit v2 on v1

v2 whole, which is shorter than its diff:
```python
import jax
import jax.numpy as jnp
from jax import lax
from jax.experimental import pallas as pl
from jax.experimental.pallas import tpu as pltpu
from jax.sharding import Mesh
from jax.sharding import PartitionSpec as P

BS = 128
ROWS = 8
CAP = 2
YCAP = 12
OWN = ROWS * CAP
LINE = ("z", "y")
ALL = ("z", "y", "x", "core")
MESH_ID = pl.DeviceIdType.MESH
ZERO = 256


def gather_kernel(x_ref, m_ref, strip, panel, smeta, pmeta, trace, s_idx, p_idx, acc, mine, plane_tr, line_tr,
                  psend, precv, xsend, xrecv, csend, crecv, lsem, asend, arecv, bsend, brecv):
    place = {a: lax.axis_index(a) for a in ("z", "y", "x")}
    after = {a: lax.rem(v + 1, 4) for a, v in place.items()}
    before = {a: lax.rem(v + 3, 4) for a, v in place.items()}
    across = {a: lax.rem(v + 2, 4) for a, v in place.items()}
    core = lax.axis_index("core")
    z, y, x = place["z"], place["y"], place["x"]
    here, line = z * 4 + y, x * 2 + core

    barrier = pltpu.get_barrier_semaphore()
    peers = [{a: to[a]} for a in ("z", "y", "x") for to in (after, before)] + [{"core": 1 - core}]
    for peer in peers:
        pl.semaphore_signal(barrier, inc=1, device_id=peer, device_id_type=MESH_ID)

    local = [
        pltpu.make_async_copy(x_ref, panel.at[here], lsem.at[0]),
        pltpu.make_async_copy(x_ref, strip.at[line], lsem.at[1]),
        pltpu.make_async_copy(m_ref, pmeta.at[here], lsem.at[2]),
        pltpu.make_async_copy(m_ref, smeta.at[line], lsem.at[3]),
    ]
    for c in local:
        c.start()
    panel[16, 0] = jnp.zeros((BS, BS), jnp.bfloat16)
    acc[...] = jnp.zeros_like(acc)
    pl.semaphore_wait(barrier, len(peers))

    sends = []

    def copy(src, dst, ss, rs, peer):
        return pltpu.make_async_remote_copy(
            src_ref=src, dst_ref=dst, send_sem=ss, recv_sem=rs, device_id=peer, device_id_type=MESH_ID
        )

    def start(*args):
        c = copy(*args)
        c.start()
        sends.append(c)

    class Ring:
        def __init__(self, axis, at, ssem, rsem, j, via=(0, 1), src=None):
            self.axis, self.at, self.ssem, self.rsem, self.j, self.via = axis, at, ssem, rsem, j, via
            self.src = src or (lambda h: at(place[axis], h))

        def order(self, q):
            return sorted(range(len(self.via)), key=lambda h: self.via[h] != q)

        def own(self, qs=(0, 1)):
            for q in qs:
                to = (after, before)[q][self.axis]
                for h in self.order(q):
                    n = q * 2 + h
                    start(self.src(h), self.at(place[self.axis], h), self.ssem.at[self.j, n], self.rsem.at[self.j, n],
                          {self.axis: to})

        def arrive(self, q):
            owner, to = (before, after)[q][self.axis], (after, before)[q][self.axis]
            for h in self.order(q):
                n, piece = q * 2 + h, self.at(owner, h)
                copy(piece, piece, self.ssem.at[self.j, n], self.rsem.at[self.j, n], {self.axis: owner}).wait_recv()
                if self.via[h] == q:
                    start(piece, piece, self.ssem.at[self.j, 4 + h], self.rsem.at[self.j, 4 + h], {self.axis: to})

        def arrive_across(self):
            for h in range(len(self.via)):
                piece = self.at(across[self.axis], h)
                copy(piece, piece, self.ssem.at[self.j, 4 + h], self.rsem.at[self.j, 4 + h],
                     {self.axis: before[self.axis]}).wait_recv()

    def chunk_of(axis, d, p):
        o = lax.rem((y if axis == "z" else z) + d, 4)
        return p * 4 + o if axis == "z" else o * 4 + p

    def panel_ring(axis, d, lo, j, via=(0, 1)):
        src = (lambda h: x_ref.at[pl.ds(lo + 4 * h, 4)]) if d == 0 else None
        return Ring(axis, lambda p, h: panel.at[chunk_of(axis, d, p), pl.ds(lo + 4 * h, 4)], psend, precv, j, via, src)

    def pmeta_ring(axis, d, j):
        src = (lambda h: m_ref) if d == 0 else None
        return Ring(axis, lambda p, h: pmeta.at[chunk_of(axis, d, p)], psend, precv, j, (0,), src)

    az, by = panel_ring("z", 0, 0, 0), panel_ring("y", 0, 8, 1)
    ay = {d: panel_ring("y", d, 0, j, v) for d, j, v in ((0, 2, (0, 1)), (1, 3, (0, 0)), (2, 4, (0, 1)), (3, 5, (1, 1)))}
    bz = {d: panel_ring("z", d, 8, j) for d, j in ((0, 6), (1, 7), (2, 8), (3, 9))}
    mz = pmeta_ring("z", 0, 10)
    my = {d: pmeta_ring("y", d, j) for d, j in ((0, 11), (1, 12), (2, 13), (3, 14))}
    xs = Ring("x", lambda p, h: strip.at[p * 2 + core, pl.ds(8 * h, 8)], xsend, xrecv, 0, (0, 1),
              lambda h: x_ref.at[pl.ds(8 * h, 8)])
    xm = Ring("x", lambda p, h: smeta.at[p * 2 + core], xsend, xrecv, 1, (0,), lambda h: m_ref)

    def swap(what, p, j, n):
        g = p * 2 + core
        start(what.at[g], what.at[g], csend.at[n, j], crecv.at[n, j], {"core": 1 - core})

    def swapped(what, p, j, n):
        g = p * 2 + 1 - core
        copy(what.at[g], what.at[g], csend.at[n, j], crecv.at[n, j], {"core": 1 - core}).wait_recv()

    source = (x == z) & (core == y // 2)
    low = lax.rem(y, 2) * 8

    def add_chunk(dz, dy):
        both = (dz, dy) not in ((0, 0), (0, 2), (2, 0), (2, 2))
        g = lax.rem(z + dz, 4) * 4 + lax.rem(y + dy, 4)
        group, base = g // 2, lax.rem(g, 2) * 8

        @pl.when(source)
        def _():
            def step(n, c):
                lefts, rights = [], []
                for u in range(4):
                    k, w = n * 2 + u // 2, u % 2
                    i = p_idx[g, 0, k * 4 + w] - low
                    ok = (w < p_idx[g, 0, k * 4 + 2]) & (i >= 0) & (i < ROWS)
                    i = jnp.clip(i, 0, ROWS - 1)
                    stored = s_idx[group, 0, i * 4 + 2]
                    first = (s_idx[group, 0, i * 4] == base + k) & (stored > 0)
                    second = (s_idx[group, 0, i * 4 + 1] == base + k) & (stored > 1)
                    sign = 1 - 2 * lax.rem(p_idx[here, 0, i * 4 + 3], 2)
                    if both:
                        sign = sign + 1 - 2 * lax.rem(p_idx[g, 0, k * 4 + 3], 2)
                    weight = jnp.where(ok & (first | second), sign, 0).astype(jnp.float32)
                    left = strip[group, i * 2 + jnp.where(second, 1, 0)]
                    lefts.append((left.astype(jnp.float32) * weight).astype(jnp.bfloat16))
                    rights.append(panel[g, k * 2 + w])
                acc[...] += jnp.dot(jnp.concatenate(lefts, axis=1), jnp.concatenate(rights, axis=0),
                                    preferred_element_type=jnp.float32)
                return c

            lax.fori_loop(0, 4, step, 0)

    mz.own()
    my[0].own()
    xm.own()
    az.own()
    by.own()
    xs.own()
    for c in local:
        c.wait()
    swap(smeta, x, 0, 1)
    swap(strip, x, 0, 0)
    for q in (0, 1):
        mz.arrive(q)
        my[0].arrive(q)
    my[1].own()
    my[3].own()
    ay[0].own()
    bz[0].own()
    for q in (0, 1):
        xm.arrive(q)
        swap(smeta, (before, after)[q]["x"], 1 + q, 1)
    for q in (0, 1):
        az.arrive(q)
        by.arrive(q)
    ay[1].own()
    bz[1].own()
    mz.arrive_across()
    my[2].own()
    my[0].arrive_across()
    xm.arrive_across()
    swap(smeta, across["x"], 3, 1)
    for d in (1, 3):
        for q in (0, 1):
            my[d].arrive(q)
    for q in (0, 1):
        xs.arrive(q)
        swap(strip, (before, after)[q]["x"], 1 + q, 0)
    az.arrive_across()
    by.arrive_across()
    ay[2].own()
    bz[2].own()
    xs.arrive_across()
    swap(strip, across["x"], 3, 0)
    ay[3].own((1,))
    ay[1].arrive(0)
    ay[1].arrive(1)
    ay[0].arrive(0)
    ay[0].arrive(1)
    for q in (0, 1):
        bz[0].arrive(q)
    for q in (0, 1):
        bz[1].arrive(q)
    for d in (1, 3):
        my[d].arrive_across()
    for q in (0, 1):
        my[2].arrive(q)
    for p, j in ((x, 0), (before["x"], 1), (after["x"], 2), (across["x"], 3)):
        swapped(smeta, p, j, 1)
        swapped(strip, p, j, 0)
    my[2].arrive_across()
    index_copies = [pltpu.make_async_copy(pmeta, p_idx, lsem.at[4]), pltpu.make_async_copy(smeta, s_idx, lsem.at[5])]
    for c in index_copies:
        c.start()
    for c in index_copies:
        c.wait()
    add_chunk(0, 0)
    add_chunk(1, 0)
    for q in (0, 1):
        ay[2].arrive(q)
        bz[2].arrive(q)
    ay[3].own((0,))
    bz[3].own()
    add_chunk(0, 1)
    add_chunk(1, 1)
    bz[0].arrive_across()
    add_chunk(2, 0)
    ay[3].arrive(1)
    add_chunk(3, 1)
    bz[1].arrive_across()
    add_chunk(2, 1)
    ay[1].arrive_across()
    add_chunk(1, 2)
    ay[0].arrive_across()
    add_chunk(0, 2)
    bz[2].arrive_across()
    ay[2].arrive_across()
    add_chunk(2, 2)

    @pl.when(source)
    def _():
        for i in range(ROWS):
            flag = lax.rem(p_idx[here, 0, i * 4 + 3], 2)
            acc[...] += (2 * flag).astype(jnp.float32) * strip[line, i * 2].astype(jnp.float32)
        eye = lax.broadcasted_iota(jnp.int32, (BS, BS), 0) == lax.broadcasted_iota(jnp.int32, (BS, BS), 1)
        total = jnp.full((1, BS), jnp.sum(jnp.where(eye, acc[...], 0.0)))
        mine[0] = total
        plane_tr[lax.rem(y, 2)] = total

    far = [(dz, dy) for dz in range(4) for dy in range(4) if dz or dy]

    def tell_plane(n):
        dz, dy = far[n]
        return copy(mine.at[0], plane_tr.at[lax.rem(y, 2)], asend.at[n], arecv.at[lax.rem(y, 2)],
                    {"z": lax.rem(z + dz, 4), "y": lax.rem(y + dy, 4)})

    @pl.when(source)
    def _():
        for n in range(len(far)):
            tell_plane(n).start()

    bz[3].arrive(0)
    bz[3].arrive(1)
    for t in range(2):
        @pl.when(jnp.logical_not(source & (lax.rem(y, 2) == t)))
        def _():
            copy(mine.at[0], plane_tr.at[t], asend.at[0], arecv.at[t], {"core": 1 - core}).wait_recv()

    total = plane_tr[0] + plane_tr[1]
    mine[1] = total
    line_tr[line] = total
    others = [(dx, dc) for dx in range(4) for dc in range(2) if dx or dc]
    for n, (dx, dc) in enumerate(others):
        start(mine.at[1], line_tr.at[line], bsend.at[n], brecv.at[line],
              {"x": lax.rem(x + dx, 4), "core": lax.rem(core + dc, 2)})
    ay[3].arrive(0)
    ay[3].arrive_across()
    bz[3].arrive_across()
    for dx, dc in others:
        g = lax.rem(x + dx, 4) * 2 + lax.rem(core + dc, 2)
        copy(mine.at[1], line_tr.at[g], bsend.at[0], brecv.at[g], {"core": 1 - core}).wait_recv()
    result = line_tr[0]
    for g in range(1, 8):
        result = result + line_tr[g]
    trace[...] = result

    @pl.when(source)
    def _():
        for n in range(len(far)):
            tell_plane(n).wait_send()

    for c in sends:
        c.wait_send()


def product_kernel(smeta, pmeta, strip, panel, out, obuf, slot, cnt, la, lb, own, osem):
    chunk = lax.axis_index("z") * 4 + lax.axis_index("y")
    mine = lax.axis_index("x") * 2 + lax.axis_index("core")

    def row(i, carry):
        packed = pmeta[chunk, 0, i * 4 + 3]
        live_y = packed // 2
        for j in range(17):
            slot[j] = YCAP
        for t in range(YCAP):
            slot[jnp.where(t < live_y, smeta[mine, 0, 32 + i * YCAP + t], 16)] = t
        slot[16] = YCAP
        for t in range(YCAP + 1):
            cnt[t] = 0
            own[t] = ZERO
            la[t, 0] = 0
            la[t, 1] = 0
            lb[t, 0] = ZERO
            lb[t, 1] = ZERO
        for q in range(CAP):
            live = q < pmeta[chunk, 0, i * 4 + 2]
            t = slot[jnp.where(live, pmeta[chunk, 0, i * 4 + q], 16)]
            own[t] = chunk * OWN + i * CAP + q

        def pairs(g, c):
            n_live = smeta[g, 0, i * 4 + 2]
            for s in range(CAP):
                @pl.when(s < n_live)
                def _():
                    k = g * 16 + smeta[g, 0, i * 4 + s]
                    kc, kr = k // 8, k % 8
                    n_in = pmeta[kc, 0, kr * 4 + 2]
                    for w in range(CAP):
                        t = slot[jnp.where(w < n_in, pmeta[kc, 0, kr * 4 + w], 16)]
                        n = cnt[t]
                        la[t, n] = g * OWN + i * CAP + s
                        lb[t, n] = k * CAP + w
                        cnt[t] = n + 1
            return c

        lax.fori_loop(0, 8, pairs, 0)
        flip = packed % 2 == 1
        sign = jnp.where(flip, -1.0, 1.0)
        twice = jnp.where(flip, 2.0, 0.0)

        def dot2(t, n):
            a = jnp.concatenate([strip[la[t, n]], strip[la[t, n + 1]]], axis=1)
            b = jnp.concatenate([panel[lb[t, n]], panel[lb[t, n + 1]]], axis=0)
            return jnp.dot(a, b, preferred_element_type=jnp.float32)

        def finish(t, product):
            return sign * product + twice * panel[own[t]].astype(jnp.float32)

        for t in range(YCAP):
            updated = finish(t, dot2(t, 0))
            obuf[i, t] = updated.astype(jnp.bfloat16)

        def more(t, c):
            n = cnt[t]

            @pl.when(n > 2)
            def _():
                la[t, n] = 0
                lb[t, n] = ZERO
                product = lax.fori_loop(
                    1, (n + 1) // 2, lambda h, acc: acc + dot2(t, h * 2), dot2(t, 0)
                )
                updated = finish(t, product)
                obuf[i, t] = updated.astype(jnp.bfloat16)

            return c

        lax.fori_loop(0, YCAP, more, 0)
        pltpu.make_async_copy(obuf.at[i], out.at[i], osem.at[i]).start()
        return carry

    lax.fori_loop(0, ROWS, row, 0)
    for i in range(ROWS):
        pltpu.make_async_copy(obuf.at[i], out.at[i], osem.at[i]).wait()


def on_device(x_blocks, x_cols, x_count, y_cols, y_count, branch_flag):
    rows = jnp.concatenate([x_cols, x_count, 2 * y_count + branch_flag[:, None]], axis=1)
    meta = jnp.concatenate([rows.reshape(1, 4 * ROWS), y_cols.reshape(1, YCAP * ROWS)], axis=1)
    vmem, hbm, smem = (pl.BlockSpec(memory_space=m) for m in (pltpu.VMEM, pltpu.HBM, pltpu.SMEM))
    dma = pltpu.SemaphoreType.DMA
    strip, panel, smeta, pmeta, trace = pl.pallas_call(
        gather_kernel,
        out_shape=[
            pltpu.VMEM((8, OWN, BS, BS), jnp.bfloat16),
            pltpu.VMEM((17, OWN, BS, BS), jnp.bfloat16),
            pltpu.VMEM((8, 1, BS), jnp.int32),
            pltpu.VMEM((16, 1, BS), jnp.int32),
            jax.ShapeDtypeStruct((1, BS), jnp.float32),
        ],
        in_specs=[hbm, vmem],
        out_specs=[vmem] * 5,
        scratch_shapes=[
            pltpu.SMEM((8, 1, BS), jnp.int32),
            pltpu.SMEM((16, 1, BS), jnp.int32),
            pltpu.VMEM((BS, BS), jnp.float32),
            pltpu.VMEM((2, 1, BS), jnp.float32),
            pltpu.VMEM((2, 1, BS), jnp.float32),
            pltpu.VMEM((8, 1, BS), jnp.float32),
            dma((15, 6)),
            dma((15, 6)),
            dma((2, 6)),
            dma((2, 6)),
            dma((2, 4)),
            dma((2, 4)),
            dma((6,)),
            dma((15,)),
            dma((2,)),
            dma((7,)),
            dma((8,)),
        ],
        compiler_params=pltpu.CompilerParams(collective_id=0, has_side_effects=True, vmem_limit_bytes=16 << 20),
    )(x_blocks.reshape(OWN, BS, BS), meta)
    out = pl.pallas_call(
        product_kernel,
        out_shape=jax.ShapeDtypeStruct((ROWS, YCAP, BS, BS), jnp.bfloat16),
        in_specs=[smem] * 2 + [vmem] * 2,
        out_specs=hbm,
        scratch_shapes=[
            pltpu.VMEM((ROWS, YCAP, BS, BS), jnp.bfloat16),
            pltpu.SMEM((17,), jnp.int32),
            pltpu.SMEM((YCAP + 1,), jnp.int32),
            pltpu.SMEM((YCAP + 1, 40), jnp.int32),
            pltpu.SMEM((YCAP + 1, 40), jnp.int32),
            pltpu.SMEM((YCAP + 1,), jnp.int32),
            dma((ROWS,)),
        ],
        compiler_params=pltpu.CompilerParams(vmem_limit_bytes=16 << 20),
    )(smeta, pmeta, strip.reshape(8 * OWN, BS, BS), panel.reshape(17 * OWN, BS, BS))
    return out, trace[0, :1]


def solution(mesh):
    finer = Mesh(mesh.devices.reshape(4, 4, 4, 2), ALL)
    placed = (
        P(LINE, ("x", "core"), None, None),
        P(LINE, ("x", "core")),
        P(LINE, ("x", "core")),
        P(LINE, ("x", "core")),
        P(LINE, ("x", "core")),
        P(LINE),
    )
    return jax.shard_map(
        on_device,
        mesh=finer,
        in_specs=placed,
        out_specs=(P(LINE, ("x", "core"), None, None), P()),
        check_vma=False,
    )
```

time: 134 us -> 81.9 us (0.61)
  blocking collectives: 65.9 us -> 0 us
  Pallas kernels: 62.6 us -> 76.6 us
  local copies, waits for them, and re-layouts: 3.8 us -> 1.97 us
    psum x1 -> x0, blocking collectives: 65.9 us -> none  [on_device(): total = lax.psum(part[0, 0], ALL)]
    pallas_call x1, Pallas kernels: 51.2 us -> 63.1 us  [on_device(): pl.pallas_call(gather_kernel, out_shape=[pltpu.VMEM((8, OWN, BS, BS), jnp...]
    pallas_call x1, Pallas kernels: 11.5 us -> 13.5 us  [on_device(): pl.pallas_call(product_kernel, out_shape=jax.ShapeDtypeStruct((ROWS, YCAP...]
    unnamed x7 -> x2, local copies, waits for them, and re-layouts: 3.11 us -> 1.04 us
where the time goes in v2:
time: 81.9 us
  Pallas kernels  76.6 us (94%)
  local copies, waits for them, and re-layouts  1.97 us (2%)
  between operations  1.81 us (2%)
  other arithmetic  1.46 us (2%)
    pallas_call x1, Pallas kernels, on_device(): pl.pallas_call(gather_kernel, out_shape=[pltpu.VMEM((8, OWN, BS, BS), jnp...  63.1 us
    pallas_call x1, Pallas kernels, on_device(): pl.pallas_call(product_kernel, out_shape=jax.ShapeDtypeStruct((ROWS, YCAP...  13.5 us

profile of v2, /device:TPU:1, one launch (start us, length us, event | category | flops | bytes accessed | tf_op | source)
XLA Modules:
  0.0 81.9 jit_solution(2784875357328945643)
XLA Ops:
  0.6 0.8 reshape.21
  1.4 0.7 bitcast_add_fusion
  2.1 0.7 pad_add_fusion
  2.8 0.1 copy.9
  2.9 0.1 reshape.20
  2.9 0.1 pad_add_fusion.1.m_ref
  3.0 0.0 copy-start
  3.0 1.0 %copy-done = bf16[8,2,128,128]{3,2,1,0:T(8,128)(2,1)S(1)} copy-done((bf16[8,2,128,128]{3,2,1,0:T(8,128)(2,1)S(1)}, bf16[8,2,128,128]{3,2,1,0:T(8,128)(2,1)}, u32[]{:S(2)}) %copy-start) | copy-done | bytes 524312
  4.1 63.1 %shard_map.77 = (bf16[8,16,128,128]{3,2,1,0:T(8,128)(2,1)S(1)}, bf16[17,16,128,128]{3,2,1,0:T(8,128)(2,1)S(1)}, s32[8,1,128]{2,1,0:T(1,128)S(1)}, s32[16,1,128]{2,1,0:T(1,128)S(1)}, f32[1,128]{1,0:T(1,128)S(1)}) custom-call(bf16[16,128,128]{2,1,0:T(8,128)(2,1)S(1)} %bitcast.9, s32[1,128]{1,0:T(1,128)S(1)} %pad_add_fusion.1.m_ref), custom_call_target="tpu_custom_call" | custom-call | tf_op jit(solution)/shard_map/pallas_call | solution.py:380
  67.1 13.5 %shard_map.78 = bf16[8,12,128,128]{3,2,1,0:T(8,128)(2,1)} custom-call(s32[8,1,128]{2,1,0:T(1,128)S(1)} %get-tuple-element.7.smeta, s32[16,1,128]{2,1,0:T(1,128)S(1)} %get-tuple-element.8.pmeta, bf16[128,128,128]{2,1,0:T(8,128)(2,1)S(1)} %bitcast.8, bf16[272,128,128]{2,1,0:T(8,128)(2,1)S(1)} %bitcast.7), custom_call_target="tpu_custom_call" | custom-call | tf_op jit(solution)/shard_map/pallas_call | solution.py:412
Async XLA Ops:
  3.0 1.0 %copy-start = (bf16[8,2,128,128]{3,2,1,0:T(8,128)(2,1)S(1)}, bf16[8,2,128,128]{3,2,1,0:T(8,128)(2,1)}, u32[]{:S(2)}) copy-start(bf16[8,2,128,128]{3,2,1,0:T(8,128)(2,1)} %param.6) | copy-start | bytes 1572868

commit v3 on v2

--- a/solution.py
+++ b/solution.py
@@ -15,9 +15,10 @@
 ALL = ("z", "y", "x", "core")
 MESH_ID = pl.DeviceIdType.MESH
 ZERO = 256
-
-
-def gather_kernel(x_ref, m_ref, strip, panel, smeta, pmeta, trace, s_idx, p_idx, acc, mine, plane_tr, line_tr,
+NONE = ZERO * 128 * 32 + 16
+
+
+def gather_kernel(x_ref, m_ref, y_ref, strip, panel, trace, table, entries, smeta, pmeta, y_mem, s_idx, p_idx, e_idx, acc, mine, plane_tr, line_tr,
                   psend, precv, xsend, xrecv, csend, crecv, lsem, asend, arecv, bsend, brecv):
     place = {a: lax.axis_index(a) for a in ("z", "y", "x")}
     after = {a: lax.rem(v + 1, 4) for a, v in place.items()}
@@ -37,6 +38,7 @@
         pltpu.make_async_copy(x_ref, strip.at[line], lsem.at[1]),
         pltpu.make_async_copy(m_ref, pmeta.at[here], lsem.at[2]),
         pltpu.make_async_copy(m_ref, smeta.at[line], lsem.at[3]),
+        pltpu.make_async_copy(y_ref, y_mem, lsem.at[7]),
     ]
     for c in local:
         c.start()
@@ -64,17 +66,17 @@
         def order(self, q):
             return sorted(range(len(self.via)), key=lambda h: self.via[h] != q)
 
-        def own(self, qs=(0, 1)):
+        def own(self, qs=(0, 1), part=slice(None)):
             for q in qs:
                 to = (after, before)[q][self.axis]
-                for h in self.order(q):
+                for h in self.order(q)[part]:
                     n = q * 2 + h
                     start(self.src(h), self.at(place[self.axis], h), self.ssem.at[self.j, n], self.rsem.at[self.j, n],
                           {self.axis: to})
 
-        def arrive(self, q):
+        def arrive(self, q, part=slice(None)):
             owner, to = (before, after)[q][self.axis], (after, before)[q][self.axis]
-            for h in self.order(q):
+            for h in self.order(q)[part]:
                 n, piece = q * 2 + h, self.at(owner, h)
                 copy(piece, piece, self.ssem.at[self.j, n], self.rsem.at[self.j, n], {self.axis: owner}).wait_recv()
                 if self.via[h] == q:
@@ -129,15 +131,15 @@
                 lefts, rights = [], []
                 for u in range(4):
                     k, w = n * 2 + u // 2, u % 2
-                    i = p_idx[g, 0, k * 4 + w] - low
-                    ok = (w < p_idx[g, 0, k * 4 + 2]) & (i >= 0) & (i < ROWS)
+                    i = p_idx[g, w, k] - low
+                    ok = (w < p_idx[g, 2, k]) & (i >= 0) & (i < ROWS)
                     i = jnp.clip(i, 0, ROWS - 1)
-                    stored = s_idx[group, 0, i * 4 + 2]
-                    first = (s_idx[group, 0, i * 4] == base + k) & (stored > 0)
-                    second = (s_idx[group, 0, i * 4 + 1] == base + k) & (stored > 1)
-                    sign = 1 - 2 * lax.rem(p_idx[here, 0, i * 4 + 3], 2)
+                    stored = s_idx[group, 2, i]
+                    first = (s_idx[group, 0, i] == base + k) & (stored > 0)
+                    second = (s_idx[group, 1, i] == base + k) & (stored > 1)
+                    sign = 1 - 2 * p_idx[here, 4, i]
                     if both:
-                        sign = sign + 1 - 2 * lax.rem(p_idx[g, 0, k * 4 + 3], 2)
+                        sign = sign + 1 - 2 * p_idx[g, 4, k]
                     weight = jnp.where(ok & (first | second), sign, 0).astype(jnp.float32)
                     left = strip[group, i * 2 + jnp.where(second, 1, 0)]
                     lefts.append((left.astype(jnp.float32) * weight).astype(jnp.bfloat16))
@@ -148,39 +150,103 @@
 
             lax.fori_loop(0, 4, step, 0)
 
+    def list_pairs():
+        def row(i, c):
+            for g in range(8):
+                stored = s_idx[g, 2, i]
+                for u in range(CAP):
+                    k = s_idx[g, u, i]
+                    chunk, r = 2 * g + k // 8, k % 8
+                    inner = jnp.where(u < stored, p_idx[chunk, 2, r], 0)
+                    for w in range(CAP):
+                        col = jnp.where(w < inner, p_idx[chunk, w, r], 16)
+                        place_b = (16 * g + k) * CAP + w
+                        e_idx[i, (g * CAP + u) * CAP + w] = (place_b * 128 + g * OWN + i * CAP + u) * 32 + col
+            return c
+
+        lax.fori_loop(0, ROWS, row, 0)
+        c = pltpu.make_async_copy(e_idx, entries, lsem.at[6])
+        c.start()
+        c.wait()
+
+    def list_slots():
+        lane = lax.broadcasted_iota(jnp.int32, (ROWS, BS), 1)
+        sub = lax.broadcasted_iota(jnp.int32, (ROWS, BS), 0)
+        entry = entries[...]
+        col = jnp.where(lane < 32, entry % 32, 16)
+        tab = jnp.zeros((ROWS, BS), jnp.int32)
+        most = jnp.zeros((ROWS, 1), jnp.int32)
+        by_row = [
+            jnp.sum(jnp.where(lane == sub, jnp.broadcast_to(m_ref[f : f + 1, :], (ROWS, BS)), 0), axis=1, keepdims=True)
+            for f in range(5)
+        ]
+        live = by_row[3]
+        for t in range(YCAP):
+            want = jnp.where(t < live, y_mem[:, t : t + 1], 17)
+            hit = (col == want).astype(jnp.int32)
+            upto = hit
+            for shift in (1, 2, 4, 8, 16):
+                upto = upto + jnp.where(lane >= shift, pltpu.roll(upto, shift, 1), 0)
+            count = jnp.sum(hit, axis=1, keepdims=True)
+            most = jnp.maximum(most, count)
+            own = jnp.full((ROWS, 1), ZERO, jnp.int32)
+            for u in range(CAP):
+                mine_u = (by_row[u] == want) & (u < by_row[2])
+                own = jnp.where(mine_u, here * OWN + sub[:, :1] * CAP + u, own)
+            values = []
+            for n in range(2):
+                found = jnp.sum(jnp.where((hit == 1) & (upto == n + 1), entry, 0), axis=1, keepdims=True)
+                values.append(jnp.where(count > n, found, NONE))
+            for f, v in enumerate((*values, count, own)):
+                tab = jnp.where(lane == t * 4 + f, v, tab)
+        tab = jnp.where(lane == 48, by_row[4], tab)
+        table[...] = jnp.where(lane == 49, most, tab)
+
+    one, two = slice(0, 1), slice(1, 2)
     mz.own()
     my[0].own()
     xm.own()
-    az.own()
-    by.own()
-    xs.own()
+    az.own(part=one)
+    by.own(part=one)
+    xs.own(part=one)
     for c in local:
         c.wait()
     swap(smeta, x, 0, 1)
-    swap(strip, x, 0, 0)
     for q in (0, 1):
         mz.arrive(q)
-        my[0].arrive(q)
     my[1].own()
     my[3].own()
-    ay[0].own()
-    bz[0].own()
-    for q in (0, 1):
+    for q in (0, 1):
+        my[0].arrive(q)
         xm.arrive(q)
+    az.own(part=two)
+    by.own(part=two)
+    xs.own(part=two)
+    for q in (0, 1):
         swap(smeta, (before, after)[q]["x"], 1 + q, 1)
-    for q in (0, 1):
-        az.arrive(q)
-        by.arrive(q)
+    swap(strip, x, 0, 0)
+    for part in (one, two):
+        ay[0].own(part=part)
+        bz[0].own(part=part)
+        if part == one:
+            mz.arrive_across()
+            my[2].own()
+            for q in (0, 1):
+                az.arrive(q, one)
+                by.arrive(q, one)
+            for d in (1, 3):
+                for q in (0, 1):
+                    my[d].arrive(q)
+    for q in (0, 1):
+        az.arrive(q, two)
+        by.arrive(q, two)
     ay[1].own()
     bz[1].own()
-    mz.arrive_across()
-    my[2].own()
     my[0].arrive_across()
+    for q in (0, 1):
+        my[2].arrive(q)
     xm.arrive_across()
     swap(smeta, across["x"], 3, 1)
-    for d in (1, 3):
-        for q in (0, 1):
-            my[d].arrive(q)
     for q in (0, 1):
         xs.arrive(q)
         swap(strip, (before, after)[q]["x"], 1 + q, 0)
@@ -188,30 +254,29 @@
     by.arrive_across()
     ay[2].own()
     bz[2].own()
+    ay[3].own((1,))
+    for d in (1, 3):
+        my[d].arrive_across()
     xs.arrive_across()
     swap(strip, across["x"], 3, 0)
-    ay[3].own((1,))
+    for q in (0, 1):
+        bz[0].arrive(q)
     ay[1].arrive(0)
     ay[1].arrive(1)
     ay[0].arrive(0)
     ay[0].arrive(1)
     for q in (0, 1):
-        bz[0].arrive(q)
-    for q in (0, 1):
         bz[1].arrive(q)
-    for d in (1, 3):
-        my[d].arrive_across()
-    for q in (0, 1):
-        my[2].arrive(q)
+    my[2].arrive_across()
     for p, j in ((x, 0), (before["x"], 1), (after["x"], 2), (across["x"], 3)):
         swapped(smeta, p, j, 1)
         swapped(strip, p, j, 0)
-    my[2].arrive_across()
     index_copies = [pltpu.make_async_copy(pmeta, p_idx, lsem.at[4]), pltpu.make_async_copy(smeta, s_idx, lsem.at[5])]
     for c in index_copies:
         c.start()
     for c in index_copies:
         c.wait()
+    list_pairs()
     add_chunk(0, 0)
     add_chunk(1, 0)
     for q in (0, 1):
@@ -219,6 +284,7 @@
         bz[2].arrive(q)
     ay[3].own((0,))
     bz[3].own()
+    list_slots()
     add_chunk(0, 1)
     add_chunk(1, 1)
     bz[0].arrive_across()
@@ -238,7 +304,7 @@
     @pl.when(source)
     def _():
         for i in range(ROWS):
-            flag = lax.rem(p_idx[here, 0, i * 4 + 3], 2)
+            flag = p_idx[here, 4, i]
             acc[...] += (2 * flag).astype(jnp.float32) * strip[line, i * 2].astype(jnp.float32)
         eye = lax.broadcasted_iota(jnp.int32, (BS, BS), 0) == lax.broadcasted_iota(jnp.int32, (BS, BS), 1)
         total = jnp.full((1, BS), jnp.sum(jnp.where(eye, acc[...], 0.0)))
@@ -257,8 +323,9 @@
         for n in range(len(far)):
             tell_plane(n).start()
 
-    bz[3].arrive(0)
-    bz[3].arrive(1)
+    for part in (one, two):
+        for q in (0, 1):
+            bz[3].arrive(q, part)
     for t in range(2):
         @pl.when(jnp.logical_not(source & (lax.rem(y, 2) == t)))
         def _():
@@ -291,79 +358,44 @@
         c.wait_send()
 
 
-def product_kernel(smeta, pmeta, strip, panel, out, obuf, slot, cnt, la, lb, own, osem):
-    chunk = lax.axis_index("z") * 4 + lax.axis_index("y")
-    mine = lax.axis_index("x") * 2 + lax.axis_index("core")
-
+def product_kernel(table, entries, strip, panel, out, obuf, found, osem):
     def row(i, carry):
-        packed = pmeta[chunk, 0, i * 4 + 3]
-        live_y = packed // 2
-        for j in range(17):
-            slot[j] = YCAP
-        for t in range(YCAP):
-            slot[jnp.where(t < live_y, smeta[mine, 0, 32 + i * YCAP + t], 16)] = t
-        slot[16] = YCAP
-        for t in range(YCAP + 1):
-            cnt[t] = 0
-            own[t] = ZERO
-            la[t, 0] = 0
-            la[t, 1] = 0
-            lb[t, 0] = ZERO
-            lb[t, 1] = ZERO
-        for q in range(CAP):
-            live = q < pmeta[chunk, 0, i * 4 + 2]
-            t = slot[jnp.where(live, pmeta[chunk, 0, i * 4 + q], 16)]
-            own[t] = chunk * OWN + i * CAP + q
-
-        def pairs(g, c):
-            n_live = smeta[g, 0, i * 4 + 2]
-            for s in range(CAP):
-                @pl.when(s < n_live)
-                def _():
-                    k = g * 16 + smeta[g, 0, i * 4 + s]
-                    kc, kr = k // 8, k % 8
-                    n_in = pmeta[kc, 0, kr * 4 + 2]
-                    for w in range(CAP):
-                        t = slot[jnp.where(w < n_in, pmeta[kc, 0, kr * 4 + w], 16)]
-                        n = cnt[t]
-                        la[t, n] = g * OWN + i * CAP + s
-                        lb[t, n] = k * CAP + w
-                        cnt[t] = n + 1
-            return c
-
-        lax.fori_loop(0, 8, pairs, 0)
-        flip = packed % 2 == 1
+        flip = table[i, 48] == 1
         sign = jnp.where(flip, -1.0, 1.0)
         twice = jnp.where(flip, 2.0, 0.0)
 
-        def dot2(t, n):
-            a = jnp.concatenate([strip[la[t, n]], strip[la[t, n + 1]]], axis=1)
-            b = jnp.concatenate([panel[lb[t, n]], panel[lb[t, n + 1]]], axis=0)
+        def dot2(c0, c1):
+            a = jnp.concatenate([strip[(c0 >> 5) & 127], strip[(c1 >> 5) & 127]], axis=1)
+            b = jnp.concatenate([panel[c0 >> 12], panel[c1 >> 12]], axis=0)
             return jnp.dot(a, b, preferred_element_type=jnp.float32)
 
         def finish(t, product):
-            return sign * product + twice * panel[own[t]].astype(jnp.float32)
+            updated = sign * product + twice * panel[table[i, t * 4 + 3]].astype(jnp.float32)
+            obuf[i, t] = updated.astype(jnp.bfloat16)
 
         for t in range(YCAP):
-            updated = finish(t, dot2(t, 0))
-            obuf[i, t] = updated.astype(jnp.bfloat16)
-
-        def more(t, c):
-            n = cnt[t]
-
-            @pl.when(n > 2)
-            def _():
-                la[t, n] = 0
-                lb[t, n] = ZERO
-                product = lax.fori_loop(
-                    1, (n + 1) // 2, lambda h, acc: acc + dot2(t, h * 2), dot2(t, 0)
-                )
-                updated = finish(t, product)
-                obuf[i, t] = updated.astype(jnp.bfloat16)
-
-            return c
-
-        lax.fori_loop(0, YCAP, more, 0)
+            finish(t, dot2(table[i, t * 4], table[i, t * 4 + 1]))
+
+        @pl.when(table[i, 49] > 2)
+        def _():
+            def more(t, c):
+                @pl.when(table[i, t * 4 + 2] > 2)
+                def _():
+                    col = table[i, t * 4] & 31
+                    n = 0
+                    for e in range(32):
+                        entry = entries[i, e]
+                        found[n] = entry
+                        n = n + jnp.where((entry & 31) == col, 1, 0)
+                    found[n] = NONE
+                    finish(t, lax.fori_loop(
+                        1, (n + 1) // 2, lambda h, p: p + dot2(found[2 * h], found[2 * h + 1]),
+                        dot2(found[0], found[1])))
+
+                return c
+
+            lax.fori_loop(0, YCAP, more, 0)
+
         pltpu.make_async_copy(obuf.at[i], out.at[i], osem.at[i]).start()
         return carry
 
@@ -373,24 +405,30 @@
 
 
 def on_device(x_blocks, x_cols, x_count, y_cols, y_count, branch_flag):
-    rows = jnp.concatenate([x_cols, x_count, 2 * y_count + branch_flag[:, None]], axis=1)
-    meta = jnp.concatenate([rows.reshape(1, 4 * ROWS), y_cols.reshape(1, YCAP * ROWS)], axis=1)
+    meta = jnp.concatenate([x_cols.T, x_count.T, y_count.T, branch_flag[None, :]], axis=0)
+    meta = jnp.pad(meta, ((0, 3), (0, BS - ROWS)))
+    x_blocks = pltpu.with_memory_space_constraint(x_blocks.reshape(OWN, BS, BS), pltpu.HBM)
+    y_cols = pltpu.with_memory_space_constraint(y_cols, pltpu.HBM)
     vmem, hbm, smem = (pl.BlockSpec(memory_space=m) for m in (pltpu.VMEM, pltpu.HBM, pltpu.SMEM))
     dma = pltpu.SemaphoreType.DMA
-    strip, panel, smeta, pmeta, trace = pl.pallas_call(
+    strip, panel, trace, table, entries = pl.pallas_call(
         gather_kernel,
         out_shape=[
             pltpu.VMEM((8, OWN, BS, BS), jnp.bfloat16),
             pltpu.VMEM((17, OWN, BS, BS), jnp.bfloat16),
-            pltpu.VMEM((8, 1, BS), jnp.int32),
-            pltpu.VMEM((16, 1, BS), jnp.int32),
             jax.ShapeDtypeStruct((1, BS), jnp.float32),
+            pltpu.VMEM((ROWS, BS), jnp.int32),
+            pltpu.VMEM((ROWS, BS), jnp.int32),
         ],
-        in_specs=[hbm, vmem],
+        in_specs=[hbm, vmem, hbm],
         out_specs=[vmem] * 5,
         scratch_shapes=[
-            pltpu.SMEM((8, 1, BS), jnp.int32),
-            pltpu.SMEM((16, 1, BS), jnp.int32),
+            pltpu.VMEM((8, ROWS, BS), jnp.int32),
+            pltpu.VMEM((16, ROWS, BS), jnp.int32),
+            pltpu.VMEM((ROWS, YCAP), jnp.int32),
+            pltpu.SMEM((8, ROWS, BS), jnp.int32),
+            pltpu.SMEM((16, ROWS, BS), jnp.int32),
+            pltpu.SMEM((ROWS, BS), jnp.int32),
             pltpu.VMEM((BS, BS), jnp.float32),
             pltpu.VMEM((2, 1, BS), jnp.float32),
             pltpu.VMEM((2, 1, BS), jnp.float32),
@@ -401,14 +439,14 @@
             dma((2, 6)),
             dma((2, 4)),
             dma((2, 4)),
-            dma((6,)),
+            dma((8,)),
             dma((15,)),
             dma((2,)),
             dma((7,)),
             dma((8,)),
         ],
         compiler_params=pltpu.CompilerParams(collective_id=0, has_side_effects=True, vmem_limit_bytes=16 << 20),
-    )(x_blocks.reshape(OWN, BS, BS), meta)
+    )(x_blocks, meta, y_cols)
     out = pl.pallas_call(
         product_kernel,
         out_shape=jax.ShapeDtypeStruct((ROWS, YCAP, BS, BS), jnp.bfloat16),
@@ -416,15 +454,11 @@
         out_specs=hbm,
         scratch_shapes=[
             pltpu.VMEM((ROWS, YCAP, BS, BS), jnp.bfloat16),
-            pltpu.SMEM((17,), jnp.int32),
-            pltpu.SMEM((YCAP + 1,), jnp.int32),
-            pltpu.SMEM((YCAP + 1, 40), jnp.int32),
-            pltpu.SMEM((YCAP + 1, 40), jnp.int32),
-            pltpu.SMEM((YCAP + 1,), jnp.int32),
+            pltpu.SMEM((40,), jnp.int32),
             dma((ROWS,)),
         ],
         compiler_params=pltpu.CompilerParams(vmem_limit_bytes=16 << 20),
-    )(smeta, pmeta, strip.reshape(8 * OWN, BS, BS), panel.reshape(17 * OWN, BS, BS))
+    )(table, entries, strip.reshape(8 * OWN, BS, BS), panel.reshape(17 * OWN, BS, BS))
     return out, trace[0, :1]
 
 

time: 81.9 us -> 67.8 us (0.83)
  Pallas kernels: 76.6 us -> 64.9 us
  local copies, waits for them, and re-layouts: 1.97 us -> 0.01 us
    pallas_call x1, Pallas kernels: 13.5 us -> 6.81 us  [on_device(): pl.pallas_call(product_kernel, out_shape=jax.ShapeDtypeStruct((ROWS, YCAP...]
    pallas_call x1, Pallas kernels: 63.1 us -> 58.1 us  [on_device(): pl.pallas_call(gather_kernel, out_shape=[pltpu.VMEM((8, OWN, BS, BS), jnp...]
    unnamed x2 -> x0, local copies, waits for them, and re-layouts: 1.04 us -> none
    reshape x2 -> x0, local copies, waits for them, and re-layouts: 0.85 us -> none  [the longest x1 0.77 us: on_device(): y_cols.reshape(1, YCAP * ROWS)]
where the time goes in v3:
time: 67.8 us; the launch traced here: 67.5 us
  Pallas kernels  64.9 us (96%)
  between operations  1.81 us (3%)
  other arithmetic  0.74 us (1%)
    pallas_call x1, Pallas kernels, on_device(): pl.pallas_call(gather_kernel, out_shape=[pltpu.VMEM((8, OWN, BS, BS), jnp...  58.1 us
    pallas_call x1, Pallas kernels, on_device(): pl.pallas_call(product_kernel, out_shape=jax.ShapeDtypeStruct((ROWS, YCAP...  6.81 us

profile of v3, /device:TPU:1, one launch (start us, length us, event | category | flops | bytes accessed | tf_op | source)
XLA Modules:
  0.0 67.5 jit_solution(748143351854851314)
XLA Ops:
  0.6 0.7 %pad_add_fusion = s32[5,8]{1,0:T(8,128)S(1)} fusion(s32[1,8]{1,0:T(1,128)} %bitcast.14, s32[1,8]{1,0:T(1,128)} %bitcast.15, s32[1,8]{1,0:T(1,128)} %bitcast.16, s32[2,8]{1,0:T(2,128)} %bitcast.13), kind=kLoop, calls=%fused_computation | loop fusion | flops 120 | bytes 320 | tf_op jit(solution)/shard_map/concatenate | solution.py:408
  1.4 58.1 %shard_map.77 = (bf16[8,16,128,128]{3,2,1,0:T(8,128)(2,1)S(1)}, bf16[17,16,128,128]{3,2,1,0:T(8,128)(2,1)S(1)}, f32[1,128]{1,0:T(1,128)S(1)}, s32[8,128]{1,0:T(8,128)S(1)}, s32[8,128]{1,0:T(8,128)S(1)}) custom-call(bf16[16,128,128]{2,1,0:T(8,128)(2,1)} %bitcast.12, s32[8,128]{1,0:T(8,128)S(1)} %pad.4.m_ref, s32[8,12]{1,0:T(8,128)} %y_ref.1), custom_call_target="tpu_custom_call" | custom-call | tf_op jit(solution)/shard_map/pallas_call | solution.py:414
  59.5 6.8 %shard_map.78 = bf16[8,12,128,128]{3,2,1,0:T(8,128)(2,1)} custom-call(s32[8,128]{1,0:T(8,128)S(1)} %get-tuple-element.7.table, s32[8,128]{1,0:T(8,128)S(1)} %get-tuple-element.8.entries, bf16[128,128,128]{2,1,0:T(8,128)(2,1)S(1)} %bitcast.10, bf16[272,128,128]{2,1,0:T(8,128)(2,1)S(1)} %bitcast.9), custom_call_target="tpu_custom_call" | custom-call | tf_op jit(solution)/shard_map/pallas_call | solution.py:450
  (1 shorter events, 0.0 us)

commit v4 on v3

--- a/solution.py
+++ b/solution.py
@@ -16,9 +16,24 @@
 MESH_ID = pl.DeviceIdType.MESH
 ZERO = 256
 NONE = ZERO * 128 * 32 + 16
-
-
-def gather_kernel(x_ref, m_ref, y_ref, strip, panel, trace, table, entries, smeta, pmeta, y_mem, s_idx, p_idx, e_idx, acc, mine, plane_tr, line_tr,
+PAIRS = 4
+WIDTH = PAIRS + 2
+FLAG = YCAP * WIDTH
+BIG = FLAG + 1
+
+
+def signs(table, i):
+    flip = table[i, FLAG] == 1
+    return jnp.where(flip, -1.0, 1.0), jnp.where(flip, 2.0, 0.0)
+
+
+def dot_pairs(strip, panel, entries):
+    a = jnp.concatenate([strip[(e >> 9) & 7, (e >> 5) & 15] for e in entries], axis=1)
+    b = jnp.concatenate([panel[e >> 16, (e >> 12) & 15] for e in entries], axis=0)
+    return jnp.dot(a, b, preferred_element_type=jnp.float32)
+
+
+def gather_kernel(x_ref, m_ref, y_ref, strip, panel, slots, trace, table, entries, smeta, pmeta, y_mem, s_idx, p_idx, e_idx, t_idx, acc, mine, plane_tr, line_tr,
                   psend, precv, xsend, xrecv, csend, crecv, lsem, asend, arecv, bsend, brecv):
     place = {a: lax.axis_index(a) for a in ("z", "y", "x")}
     after = {a: lax.rem(v + 1, 4) for a, v in place.items()}
@@ -74,13 +89,18 @@
                     start(self.src(h), self.at(place[self.axis], h), self.ssem.at[self.j, n], self.rsem.at[self.j, n],
                           {self.axis: to})
 
-        def arrive(self, q, part=slice(None)):
-            owner, to = (before, after)[q][self.axis], (after, before)[q][self.axis]
+        def arrive(self, q, part=slice(None), hold=()):
+            owner = (before, after)[q][self.axis]
             for h in self.order(q)[part]:
                 n, piece = q * 2 + h, self.at(owner, h)
                 copy(piece, piece, self.ssem.at[self.j, n], self.rsem.at[self.j, n], {self.axis: owner}).wait_recv()
-                if self.via[h] == q:
-                    start(piece, piece, self.ssem.at[self.j, 4 + h], self.rsem.at[self.j, 4 + h], {self.axis: to})
+                if self.via[h] == q and h not in hold:
+                    self.pass_on(q, h)
+
+        def pass_on(self, q, h):
+            piece = self.at((before, after)[q][self.axis], h)
+            start(piece, piece, self.ssem.at[self.j, 4 + h], self.rsem.at[self.j, 4 + h],
+                  {self.axis: (after, before)[q][self.axis]})
 
         def arrive_across(self):
             for h in range(len(self.via)):
@@ -175,7 +195,7 @@
         entry = entries[...]
         col = jnp.where(lane < 32, entry % 32, 16)
         tab = jnp.zeros((ROWS, BS), jnp.int32)
-        most = jnp.zeros((ROWS, 1), jnp.int32)
+        big = jnp.zeros((ROWS, 1), jnp.int32)
         by_row = [
             jnp.sum(jnp.where(lane == sub, jnp.broadcast_to(m_ref[f : f + 1, :], (ROWS, BS)), 0), axis=1, keepdims=True)
             for f in range(5)
@@ -188,19 +208,34 @@
             for shift in (1, 2, 4, 8, 16):
                 upto = upto + jnp.where(lane >= shift, pltpu.roll(upto, shift, 1), 0)
             count = jnp.sum(hit, axis=1, keepdims=True)
-            most = jnp.maximum(most, count)
             own = jnp.full((ROWS, 1), ZERO, jnp.int32)
             for u in range(CAP):
                 mine_u = (by_row[u] == want) & (u < by_row[2])
                 own = jnp.where(mine_u, here * OWN + sub[:, :1] * CAP + u, own)
-            values = []
-            for n in range(2):
+            for n in range(PAIRS):
                 found = jnp.sum(jnp.where((hit == 1) & (upto == n + 1), entry, 0), axis=1, keepdims=True)
-                values.append(jnp.where(count > n, found, NONE))
-            for f, v in enumerate((*values, count, own)):
-                tab = jnp.where(lane == t * 4 + f, v, tab)
-        tab = jnp.where(lane == 48, by_row[4], tab)
-        table[...] = jnp.where(lane == 49, most, tab)
+                tab = jnp.where(lane == t * WIDTH + n, jnp.where(count > n, found, NONE), tab)
+            tab = jnp.where(lane == t * WIDTH + PAIRS, count, tab)
+            tab = jnp.where(lane == t * WIDTH + PAIRS + 1, own, tab)
+            tab = jnp.where((lane == BIG + 1 + big) & (count > 2), t, tab)
+            big = big + jnp.where(count > 2, 1, 0)
+        tab = jnp.where(lane == FLAG, by_row[4], tab)
+        table[...] = jnp.where(lane == BIG, big, tab)
+        c = pltpu.make_async_copy(table, t_idx, lsem.at[8])
+        c.start()
+        c.wait()
+
+    def multiply(first, last):
+        def row(i, c):
+            sign, twice = signs(t_idx, i)
+            for t in range(YCAP):
+                product = dot_pairs(strip, panel, [t_idx[i, t * WIDTH + n] for n in range(2)])
+                own = t_idx[i, t * WIDTH + PAIRS + 1]
+                updated = sign * product + twice * panel[own >> 4, own & 15].astype(jnp.float32)
+                slots[i, t] = updated.astype(jnp.bfloat16)
+            return c
+
+        lax.fori_loop(first, last, row, 0)
 
     one, two = slice(0, 1), slice(1, 2)
     mz.own()
@@ -282,14 +317,14 @@
     for q in (0, 1):
         ay[2].arrive(q)
         bz[2].arrive(q)
-    ay[3].own((0,))
+    ay[3].own((0,), one)
     bz[3].own()
     list_slots()
     add_chunk(0, 1)
     add_chunk(1, 1)
     bz[0].arrive_across()
     add_chunk(2, 0)
-    ay[3].arrive(1)
+    ay[3].arrive(1, hold=(1,))
     add_chunk(3, 1)
     bz[1].arrive_across()
     add_chunk(2, 1)
@@ -323,6 +358,9 @@
         for n in range(len(far)):
             tell_plane(n).start()
 
+    ay[3].own((0,), two)
+    ay[3].pass_on(1, 1)
+
     for part in (one, two):
         for q in (0, 1):
             bz[3].arrive(q, part)
@@ -341,6 +379,7 @@
     ay[3].arrive(0)
     ay[3].arrive_across()
     bz[3].arrive_across()
+    multiply(0, ROWS)
     for dx, dc in others:
         g = lax.rem(x + dx, 4) * 2 + lax.rem(core + dc, 2)
         copy(mine.at[1], line_tr.at[g], bsend.at[0], brecv.at[g], {"core": 1 - core}).wait_recv()
@@ -358,50 +397,67 @@
         c.wait_send()
 
 
-def product_kernel(table, entries, strip, panel, out, obuf, found, osem):
+def finish_kernel(table, entries, strip, panel, slots, out, redone, found, osem):
+    for i in range(ROWS):
+        @pl.when(table[i, BIG] == 0)
+        def _():
+            pltpu.make_async_copy(slots.at[i], out.at[i], osem.at[i]).start()
+
+    def redo(i, t):
+        count = table[i, t * WIDTH + PAIRS]
+        sign, twice = signs(table, i)
+        own = table[i, t * WIDTH + PAIRS + 1]
+
+        def store(product):
+            updated = sign * product + twice * panel[own >> 4, own & 15].astype(jnp.float32)
+            redone[i, t] = updated.astype(jnp.bfloat16)
+
+        @pl.when(count <= PAIRS)
+        def _():
+            store(dot_pairs(strip, panel, [table[i, t * WIDTH + n] for n in range(PAIRS)]))
+
+        @pl.when(count > PAIRS)
+        def _():
+            col = table[i, t * WIDTH] & 31
+            n = 0
+            for e in range(32):
+                entry = entries[i, e]
+                found[n] = entry
+                n = n + jnp.where((entry & 31) == col, 1, 0)
+            found[n] = NONE
+            store(lax.fori_loop(
+                1, (n + 1) // 2, lambda h, p: p + dot_pairs(strip, panel, [found[2 * h], found[2 * h + 1]]),
+                dot_pairs(strip, panel, [found[0], found[1]])))
+
     def row(i, carry):
-        flip = table[i, 48] == 1
-        sign = jnp.where(flip, -1.0, 1.0)
-        twice = jnp.where(flip, 2.0, 0.0)
-
-        def dot2(c0, c1):
-            a = jnp.concatenate([strip[(c0 >> 5) & 127], strip[(c1 >> 5) & 127]], axis=1)
-            b = jnp.concatenate([panel[c0 >> 12], panel[c1 >> 12]], axis=0)
-            return jnp.dot(a, b, preferred_element_type=jnp.float32)
-
-        def finish(t, product):
-            updated = sign * product + twice * panel[table[i, t * 4 + 3]].astype(jnp.float32)
-            obuf[i, t] = updated.astype(jnp.bfloat16)
-
-        for t in range(YCAP):
-            finish(t, dot2(table[i, t * 4], table[i, t * 4 + 1]))
-
-        @pl.when(table[i, 49] > 2)
+        @pl.when(table[i, BIG] > 0)
         def _():
-            def more(t, c):
-                @pl.when(table[i, t * 4 + 2] > 2)
+            def again(n, c):
+                redo(i, table[i, BIG + 1 + n])
+                return c
+
+            lax.fori_loop(0, table[i, BIG], again, 0)
+
+            def send(t, c):
+                big = table[i, t * WIDTH + PAIRS] > 2
+
+                @pl.when(big)
                 def _():
-                    col = table[i, t * 4] & 31
-                    n = 0
-                    for e in range(32):
-                        entry = entries[i, e]
-                        found[n] = entry
-                        n = n + jnp.where((entry & 31) == col, 1, 0)
-                    found[n] = NONE
-                    finish(t, lax.fori_loop(
-                        1, (n + 1) // 2, lambda h, p: p + dot2(found[2 * h], found[2 * h + 1]),
-                        dot2(found[0], found[1])))
+                    pltpu.make_async_copy(redone.at[i, t], out.at[i, t], osem.at[i]).start()
+
+                @pl.when(jnp.logical_not(big))
+                def _():
+                    pltpu.make_async_copy(slots.at[i, t], out.at[i, t], osem.at[i]).start()
 
                 return c
 
-            lax.fori_loop(0, YCAP, more, 0)
-
-        pltpu.make_async_copy(obuf.at[i], out.at[i], osem.at[i]).start()
+            lax.fori_loop(0, YCAP, send, 0)
+
         return carry
 
     lax.fori_loop(0, ROWS, row, 0)
     for i in range(ROWS):
-        pltpu.make_async_copy(obuf.at[i], out.at[i], osem.at[i]).wait()
+        pltpu.make_async_copy(slots.at[i], out.at[i], osem.at[i]).wait()
 
 
 def on_device(x_blocks, x_cols, x_count, y_cols, y_count, branch_flag):
@@ -411,23 +467,25 @@
     y_cols = pltpu.with_memory_space_constraint(y_cols, pltpu.HBM)
     vmem, hbm, smem = (pl.BlockSpec(memory_space=m) for m in (pltpu.VMEM, pltpu.HBM, pltpu.SMEM))
     dma = pltpu.SemaphoreType.DMA
-    strip, panel, trace, table, entries = pl.pallas_call(
+    strip, panel, slots, trace, table, entries = pl.pallas_call(
         gather_kernel,
         out_shape=[
             pltpu.VMEM((8, OWN, BS, BS), jnp.bfloat16),
             pltpu.VMEM((17, OWN, BS, BS), jnp.bfloat16),
+            pltpu.VMEM((ROWS, YCAP, BS, BS), jnp.bfloat16),
             jax.ShapeDtypeStruct((1, BS), jnp.float32),
             pltpu.VMEM((ROWS, BS), jnp.int32),
             pltpu.VMEM((ROWS, BS), jnp.int32),
         ],
         in_specs=[hbm, vmem, hbm],
-        out_specs=[vmem] * 5,
+        out_specs=[vmem] * 6,
         scratch_shapes=[
             pltpu.VMEM((8, ROWS, BS), jnp.int32),
             pltpu.VMEM((16, ROWS, BS), jnp.int32),
             pltpu.VMEM((ROWS, YCAP), jnp.int32),
             pltpu.SMEM((8, ROWS, BS), jnp.int32),
             pltpu.SMEM((16, ROWS, BS), jnp.int32),
+            pltpu.SMEM((ROWS, BS), jnp.int32),
             pltpu.SMEM((ROWS, BS), jnp.int32),
             pltpu.VMEM((BS, BS), jnp.float32),
             pltpu.VMEM((2, 1, BS), jnp.float32),
@@ -439,7 +497,7 @@
             dma((2, 6)),
             dma((2, 4)),
             dma((2, 4)),
-            dma((8,)),
+            dma((9,)),
             dma((15,)),
             dma((2,)),
             dma((7,)),
@@ -448,9 +506,9 @@
         compiler_params=pltpu.CompilerParams(collective_id=0, has_side_effects=True, vmem_limit_bytes=16 << 20),
     )(x_blocks, meta, y_cols)
     out = pl.pallas_call(
-        product_kernel,
+        finish_kernel,
         out_shape=jax.ShapeDtypeStruct((ROWS, YCAP, BS, BS), jnp.bfloat16),
-        in_specs=[smem] * 2 + [vmem] * 2,
+        in_specs=[smem] * 2 + [vmem] * 3,
         out_specs=hbm,
         scratch_shapes=[
             pltpu.VMEM((ROWS, YCAP, BS, BS), jnp.bfloat16),
@@ -458,7 +516,7 @@
             dma((ROWS,)),
         ],
         compiler_params=pltpu.CompilerParams(vmem_limit_bytes=16 << 20),
-    )(table, entries, strip.reshape(8 * OWN, BS, BS), panel.reshape(17 * OWN, BS, BS))
+    )(table, entries, strip, panel, slots)
     return out, trace[0, :1]
 
 

time: 67.8 us -> 64.3 us (0.948)
  Pallas kernels: 64.9 us -> 61.4 us
    pallas_call x1, Pallas kernels: 6.81 us -> 3.27 us  [on_device(): pl.pallas_call(finish_kernel, out_shape=jax.ShapeDtypeStruct((ROWS, YCAP,...]
where the time goes in v4:
time: 64.3 us; the launch traced here: 63.9 us
  Pallas kernels  61.4 us (95%)
  between operations  1.81 us (3%)
  other arithmetic  0.74 us (1%)
    pallas_call x1, Pallas kernels, on_device(): pl.pallas_call(gather_kernel, out_shape=[pltpu.VMEM((8, OWN, BS, BS), jnp...  58.1 us
    pallas_call x1, Pallas kernels, on_device(): pl.pallas_call(finish_kernel, out_shape=jax.ShapeDtypeStruct((ROWS, YCAP,...  3.27 us

profile of v4, /device:TPU:1, one launch (start us, length us, event | category | flops | bytes accessed | tf_op | source)
XLA Modules:
  0.0 63.9 jit_solution(10578748341801369570)
XLA Ops:
  0.6 0.7 %pad_add_fusion = s32[5,8]{1,0:T(8,128)S(1)} fusion(s32[1,8]{1,0:T(1,128)} %bitcast.10, s32[1,8]{1,0:T(1,128)} %bitcast.11, s32[1,8]{1,0:T(1,128)} %bitcast.12, s32[2,8]{1,0:T(2,128)} %bitcast.9), kind=kLoop, calls=%fused_computation | loop fusion | flops 120 | bytes 320 | tf_op jit(solution)/shard_map/concatenate | solution.py:464
  1.4 58.1 %shard_map.77 = (bf16[8,16,128,128]{3,2,1,0:T(8,128)(2,1)S(1)}, bf16[17,16,128,128]{3,2,1,0:T(8,128)(2,1)S(1)}, bf16[8,12,128,128]{3,2,1,0:T(8,128)(2,1)S(1)}, f...) custom-call(bf16[16,128,128]{2,1,0:T(8,128)(2,1)} %bitcast.8, s32[8,128]{1,0:T(8,128)S(1)} %pad.4.m_ref, ...), custom_call_target="tpu_custom_call" | custom-call | tf_op jit(solution)/shard_map/pallas_call | solution.py:470
  59.5 3.3 %shard_map.78 = bf16[8,12,128,128]{3,2,1,0:T(8,128)(2,1)} custom-call(s32[8,128]{1,0:T(8,128)S(1)} %get-tuple-element.8.table, s32[8,128]{1,0:T(8,128)S(1)} %get-tuple-element.9.entries, bf16[8,16,128,128]{3,2,1,0:T(8,128)(2,1)S(1)} %get-tuple-element.10.strip, bf16[17,16,128,128]{3,2,1,0:T(8,128)(2,1)S(1)} %get-tuple-element.11.panel, ...), custom_call_target="tpu_custom_call" | custom-call | tf_op jit(solution)/shard_map/pallas_call | solution.py:508
  (1 shorter events, 0.0 us)

commit v5 on v4

--- a/solution.py
+++ b/solution.py
@@ -33,8 +33,10 @@
     return jnp.dot(a, b, preferred_element_type=jnp.float32)
 
 
-def gather_kernel(x_ref, m_ref, y_ref, strip, panel, slots, trace, table, entries, smeta, pmeta, y_mem, s_idx, p_idx, e_idx, t_idx, acc, mine, plane_tr, line_tr,
-                  psend, precv, xsend, xrecv, csend, crecv, lsem, asend, arecv, bsend, brecv):
+def gather_kernel(x_ref, *refs):
+    (cols_ref, x_count_ref, y_count_ref, flag_ref, y_ref, strip, panel, slots, trace, table, entries, smeta, pmeta,
+     m_ref, cols_mem, x_count_mem, y_count_mem, flag_mem, y_mem, s_idx, p_idx, e_idx, t_idx, acc, mine, plane_tr, line_tr,
+     psend, precv, xsend, xrecv, csend, crecv, lsem, msem, asend, arecv, bsend, brecv) = refs
     place = {a: lax.axis_index(a) for a in ("z", "y", "x")}
     after = {a: lax.rem(v + 1, 4) for a, v in place.items()}
     before = {a: lax.rem(v + 3, 4) for a, v in place.items()}
@@ -51,12 +53,17 @@
     local = [
         pltpu.make_async_copy(x_ref, panel.at[here], lsem.at[0]),
         pltpu.make_async_copy(x_ref, strip.at[line], lsem.at[1]),
-        pltpu.make_async_copy(m_ref, pmeta.at[here], lsem.at[2]),
-        pltpu.make_async_copy(m_ref, smeta.at[line], lsem.at[3]),
         pltpu.make_async_copy(y_ref, y_mem, lsem.at[7]),
     ]
-    for c in local:
+    fields = ((cols_ref, cols_mem), (x_count_ref, x_count_mem), (y_count_ref, y_count_mem), (flag_ref, flag_mem))
+    small = [pltpu.make_async_copy(a, b, msem.at[n]) for n, (a, b) in enumerate(fields)]
+    for c in small + local:
         c.start()
+    for c in small:
+        c.wait()
+    for row, (_, b) in zip((0, 2, 3, 4), fields):
+        for tile in (m_ref, smeta.at[line], pmeta.at[here]):
+            tile[row : row + b.shape[0], :ROWS] = b[...]
     panel[16, 0] = jnp.zeros((BS, BS), jnp.bfloat16)
     acc[...] = jnp.zeros_like(acc)
     pl.semaphore_wait(barrier, len(peers))
@@ -312,6 +319,13 @@
     for c in index_copies:
         c.wait()
     list_pairs()
+
+    @pl.when(source)
+    def _():
+        for i in range(ROWS):
+            flag = p_idx[here, 4, i]
+            acc[...] += (2 * flag).astype(jnp.float32) * strip[line, i * 2].astype(jnp.float32)
+
     add_chunk(0, 0)
     add_chunk(1, 0)
     for q in (0, 1):
@@ -338,15 +352,12 @@
 
     @pl.when(source)
     def _():
-        for i in range(ROWS):
-            flag = p_idx[here, 4, i]
-            acc[...] += (2 * flag).astype(jnp.float32) * strip[line, i * 2].astype(jnp.float32)
         eye = lax.broadcasted_iota(jnp.int32, (BS, BS), 0) == lax.broadcasted_iota(jnp.int32, (BS, BS), 1)
         total = jnp.full((1, BS), jnp.sum(jnp.where(eye, acc[...], 0.0)))
         mine[0] = total
         plane_tr[lax.rem(y, 2)] = total
 
-    far = [(dz, dy) for dz in range(4) for dy in range(4) if dz or dy]
+    far = [(dz, dy) for dz in (2, 1, 3, 0) for dy in (2, 1, 3, 0) if dz or dy]
 
     def tell_plane(n):
         dz, dy = far[n]
@@ -372,7 +383,7 @@
     total = plane_tr[0] + plane_tr[1]
     mine[1] = total
     line_tr[line] = total
-    others = [(dx, dc) for dx in range(4) for dc in range(2) if dx or dc]
+    others = [(dx, dc) for dx in (2, 1, 3, 0) for dc in (1, 0) if dx or dc]
     for n, (dx, dc) in enumerate(others):
         start(mine.at[1], line_tr.at[line], bsend.at[n], brecv.at[line],
               {"x": lax.rem(x + dx, 4), "core": lax.rem(core + dc, 2)})
@@ -461,10 +472,11 @@
 
 
 def on_device(x_blocks, x_cols, x_count, y_cols, y_count, branch_flag):
-    meta = jnp.concatenate([x_cols.T, x_count.T, y_count.T, branch_flag[None, :]], axis=0)
-    meta = jnp.pad(meta, ((0, 3), (0, BS - ROWS)))
     x_blocks = pltpu.with_memory_space_constraint(x_blocks.reshape(OWN, BS, BS), pltpu.HBM)
-    y_cols = pltpu.with_memory_space_constraint(y_cols, pltpu.HBM)
+    indices = [
+        pltpu.with_memory_space_constraint(a, pltpu.HBM)
+        for a in (x_cols.T, x_count.T, y_count.T, branch_flag[None, :], y_cols)
+    ]
     vmem, hbm, smem = (pl.BlockSpec(memory_space=m) for m in (pltpu.VMEM, pltpu.HBM, pltpu.SMEM))
     dma = pltpu.SemaphoreType.DMA
     strip, panel, slots, trace, table, entries = pl.pallas_call(
@@ -477,11 +489,16 @@
             pltpu.VMEM((ROWS, BS), jnp.int32),
             pltpu.VMEM((ROWS, BS), jnp.int32),
         ],
-        in_specs=[hbm, vmem, hbm],
+        in_specs=[hbm] * 6,
         out_specs=[vmem] * 6,
         scratch_shapes=[
             pltpu.VMEM((8, ROWS, BS), jnp.int32),
             pltpu.VMEM((16, ROWS, BS), jnp.int32),
+            pltpu.VMEM((ROWS, BS), jnp.int32),
+            pltpu.VMEM((CAP, ROWS), jnp.int32),
+            pltpu.VMEM((1, ROWS), jnp.int32),
+            pltpu.VMEM((1, ROWS), jnp.int32),
+            pltpu.VMEM((1, ROWS), jnp.int32),
             pltpu.VMEM((ROWS, YCAP), jnp.int32),
             pltpu.SMEM((8, ROWS, BS), jnp.int32),
             pltpu.SMEM((16, ROWS, BS), jnp.int32),
@@ -498,13 +515,14 @@
             dma((2, 4)),
             dma((2, 4)),
             dma((9,)),
+            dma((4,)),
             dma((15,)),
             dma((2,)),
             dma((7,)),
             dma((8,)),
         ],
         compiler_params=pltpu.CompilerParams(collective_id=0, has_side_effects=True, vmem_limit_bytes=16 << 20),
-    )(x_blocks, meta, y_cols)
+    )(x_blocks, *indices)
     out = pl.pallas_call(
         finish_kernel,
         out_shape=jax.ShapeDtypeStruct((ROWS, YCAP, BS, BS), jnp.bfloat16),

time: 64.3 us -> 63 us (0.980)
  other arithmetic: 0.74 us -> 0 us
    concatenate x1 -> x0, other arithmetic: 0.74 us -> none  [on_device(): jnp.concatenate([x_cols.T, x_count.T, y_count.T, branch_flag[None, :]], a...]
where the time goes in v5:
time: 63 us; the launch traced here: 62.8 us
  Pallas kernels  61 us (97%)
  between operations  1.81 us (3%)
    pallas_call x1, Pallas kernels, on_device(): pl.pallas_call(gather_kernel, out_shape=[pltpu.VMEM((8, OWN, BS, BS), jnp...  58.1 us
    pallas_call x1, Pallas kernels, on_device(): pl.pallas_call(finish_kernel, out_shape=jax.ShapeDtypeStruct((ROWS, YCAP,...  2.9 us

profile of v5, /device:TPU:1, one launch (start us, length us, event | category | flops | bytes accessed | tf_op | source)
XLA Modules:
  0.0 62.8 jit_solution(1262874555776810983)
XLA Ops:
  0.6 58.1 %shard_map.77 = (bf16[8,16,128,128]{3,2,1,0:T(8,128)(2,1)S(1)}, bf16[17,16,128,128]{3,2,1,0:T(8,128)(2,1)S(1)}, bf16[8,12,128,128]{3,2,1,0:T(8,128)(2,1)S(1)}, f...) custom-call(bf16[16,128,128]{2,1,0:T(8,128)(2,1)} %bitcast.8, s32[2,8]{1,0:T(2,128)} %bitcast.9, ...), custom_call_target="tpu_custom_call" | custom-call | tf_op jit(solution)/shard_map/pallas_call | solution.py:482
  58.7 2.9 %shard_map.78 = bf16[8,12,128,128]{3,2,1,0:T(8,128)(2,1)} custom-call(s32[8,128]{1,0:T(8,128)S(1)} %get-tuple-element.8.table, s32[8,128]{1,0:T(8,128)S(1)} %get-tuple-element.9.entries, bf16[8,16,128,128]{3,2,1,0:T(8,128)(2,1)S(1)} %get-tuple-element.10.strip, bf16[17,16,128,128]{3,2,1,0:T(8,128)(2,1)S(1)} %get-tuple-element.11.panel, ...), custom_call_target="tpu_custom_call" | custom-call | tf_op jit(solution)/shard_map/pallas_call | solution.py:526

commit v6 on v5

--- a/solution.py
+++ b/solution.py
@@ -166,13 +166,14 @@
                     second = (s_idx[group, 1, i] == base + k) & (stored > 1)
                     sign = 1 - 2 * p_idx[here, 4, i]
                     if both:
-                        sign = sign + 1 - 2 * p_idx[g, 4, k]
+                        sign = jnp.where(p_idx[g, 4, k] == p_idx[here, 4, i], sign, 0)
                     weight = jnp.where(ok & (first | second), sign, 0).astype(jnp.float32)
                     left = strip[group, i * 2 + jnp.where(second, 1, 0)]
                     lefts.append((left.astype(jnp.float32) * weight).astype(jnp.bfloat16))
                     rights.append(panel[g, k * 2 + w])
-                acc[...] += jnp.dot(jnp.concatenate(lefts, axis=1), jnp.concatenate(rights, axis=0),
-                                    preferred_element_type=jnp.float32)
+                product = jnp.dot(jnp.concatenate(lefts, axis=1), jnp.concatenate(rights, axis=0),
+                                  preferred_element_type=jnp.float32)
+                acc[...] += 2.0 * product if both else product
                 return c
 
             lax.fori_loop(0, 4, step, 0)
@@ -391,6 +392,14 @@
     ay[3].arrive_across()
     bz[3].arrive_across()
     multiply(0, ROWS)
+    @pl.when(source)
+    def _():
+        for n in range(len(far)):
+            tell_plane(n).wait_send()
+
+    for c in sends:
+        c.wait_send()
+
     for dx, dc in others:
         g = lax.rem(x + dx, 4) * 2 + lax.rem(core + dc, 2)
         copy(mine.at[1], line_tr.at[g], bsend.at[0], brecv.at[g], {"core": 1 - core}).wait_recv()
@@ -398,14 +407,6 @@
     for g in range(1, 8):
         result = result + line_tr[g]
     trace[...] = result
-
-    @pl.when(source)
-    def _():
-        for n in range(len(far)):
-            tell_plane(n).wait_send()
-
-    for c in sends:
-        c.wait_send()
 
 
 def finish_kernel(table, entries, strip, panel, slots, out, redone, found, osem):

time: 63 us -> 62.5 us (level)
  no operation moved by 1% of the time
where the time goes in v6:
time: 62.5 us; the launch traced here: 62.7 us
  Pallas kernels  60.9 us (97%)
  between operations  1.81 us (3%)
    pallas_call x1, Pallas kernels, on_device(): pl.pallas_call(gather_kernel, out_shape=[pltpu.VMEM((8, OWN, BS, BS), jnp...  57.9 us
    pallas_call x1, Pallas kernels, on_device(): pl.pallas_call(finish_kernel, out_shape=jax.ShapeDtypeStruct((ROWS, YCAP,...  2.93 us

profile of v6, /device:TPU:1, one launch (start us, length us, event | category | flops | bytes accessed | tf_op | source)
XLA Modules:
  0.0 62.7 jit_solution(17246754198593187541)
XLA Ops:
  0.6 57.9 %shard_map.77 = (bf16[8,16,128,128]{3,2,1,0:T(8,128)(2,1)S(1)}, bf16[17,16,128,128]{3,2,1,0:T(8,128)(2,1)S(1)}, bf16[8,12,128,128]{3,2,1,0:T(8,128)(2,1)S(1)}, f...) custom-call(bf16[16,128,128]{2,1,0:T(8,128)(2,1)} %bitcast.8, s32[2,8]{1,0:T(2,128)} %bitcast.9, ...), custom_call_target="tpu_custom_call" | custom-call | tf_op jit(solution)/shard_map/pallas_call | solution.py:483
  58.6 2.9 %shard_map.78 = bf16[8,12,128,128]{3,2,1,0:T(8,128)(2,1)} custom-call(s32[8,128]{1,0:T(8,128)S(1)} %get-tuple-element.8.table, s32[8,128]{1,0:T(8,128)S(1)} %get-tuple-element.9.entries, bf16[8,16,128,128]{3,2,1,0:T(8,128)(2,1)S(1)} %get-tuple-element.10.strip, bf16[17,16,128,128]{3,2,1,0:T(8,128)(2,1)S(1)} %get-tuple-element.11.panel, ...), custom_call_target="tpu_custom_call" | custom-call | tf_op jit(solution)/shard_map/pallas_call | solution.py:527

commit v7 on v6

--- a/solution.py
+++ b/solution.py
@@ -16,6 +16,7 @@
 MESH_ID = pl.DeviceIdType.MESH
 ZERO = 256
 NONE = ZERO * 128 * 32 + 16
+DIRECT = 3
 PAIRS = 4
 WIDTH = PAIRS + 2
 FLAG = YCAP * WIDTH
@@ -225,8 +226,8 @@
                 tab = jnp.where(lane == t * WIDTH + n, jnp.where(count > n, found, NONE), tab)
             tab = jnp.where(lane == t * WIDTH + PAIRS, count, tab)
             tab = jnp.where(lane == t * WIDTH + PAIRS + 1, own, tab)
-            tab = jnp.where((lane == BIG + 1 + big) & (count > 2), t, tab)
-            big = big + jnp.where(count > 2, 1, 0)
+            tab = jnp.where((lane == BIG + 1 + big) & (count > DIRECT), t, tab)
+            big = big + jnp.where(count > DIRECT, 1, 0)
         tab = jnp.where(lane == FLAG, by_row[4], tab)
         table[...] = jnp.where(lane == BIG, big, tab)
         c = pltpu.make_async_copy(table, t_idx, lsem.at[8])
@@ -237,13 +238,18 @@
         def row(i, c):
             sign, twice = signs(t_idx, i)
             for t in range(YCAP):
-                product = dot_pairs(strip, panel, [t_idx[i, t * WIDTH + n] for n in range(2)])
+                product = dot_pairs(strip, panel, [t_idx[i, t * WIDTH + n] for n in range(DIRECT)])
                 own = t_idx[i, t * WIDTH + PAIRS + 1]
                 updated = sign * product + twice * panel[own >> 4, own & 15].astype(jnp.float32)
                 slots[i, t] = updated.astype(jnp.bfloat16)
             return c
 
-        lax.fori_loop(first, last, row, 0)
+        def rows(n, c):
+            for u in range(4):
+                row(n * 4 + u, c)
+            return c
+
+        lax.fori_loop(first // 4, last // 4, rows, 0)
 
     one, two = slice(0, 1), slice(1, 2)
     mz.own()
@@ -451,7 +457,7 @@
             lax.fori_loop(0, table[i, BIG], again, 0)
 
             def send(t, c):
-                big = table[i, t * WIDTH + PAIRS] > 2
+                big = table[i, t * WIDTH + PAIRS] > DIRECT
 
                 @pl.when(big)
                 def _():

time: 62.5 us -> 62.3 us (level)
  no operation moved by 1% of the time
where the time goes in v7:
time: 62.3 us; the launch traced here: 62.1 us
  Pallas kernels  60.3 us (97%)
  between operations  1.81 us (3%)
    pallas_call x1, Pallas kernels, on_device(): pl.pallas_call(gather_kernel, out_shape=[pltpu.VMEM((8, OWN, BS, BS), jnp...  57.9 us
    pallas_call x1, Pallas kernels, on_device(): pl.pallas_call(finish_kernel, out_shape=jax.ShapeDtypeStruct((ROWS, YCAP,...  2.39 us

profile of v7, /device:TPU:1, one launch (start us, length us, event | category | flops | bytes accessed | tf_op | source)
XLA Modules:
  0.0 62.1 jit_solution(117855128708021584)
XLA Ops:
  0.6 57.9 %shard_map.77 = (bf16[8,16,128,128]{3,2,1,0:T(8,128)(2,1)S(1)}, bf16[17,16,128,128]{3,2,1,0:T(8,128)(2,1)S(1)}, bf16[8,12,128,128]{3,2,1,0:T(8,128)(2,1)S(1)}, f...) custom-call(bf16[16,128,128]{2,1,0:T(8,128)(2,1)} %bitcast.8, s32[2,8]{1,0:T(2,128)} %bitcast.9, ...), custom_call_target="tpu_custom_call" | custom-call | tf_op jit(solution)/shard_map/pallas_call | solution.py:489
  58.6 2.4 %shard_map.78 = bf16[8,12,128,128]{3,2,1,0:T(8,128)(2,1)} custom-call(s32[8,128]{1,0:T(8,128)S(1)} %get-tuple-element.8.table, s32[8,128]{1,0:T(8,128)S(1)} %get-tuple-element.9.entries, bf16[8,16,128,128]{3,2,1,0:T(8,128)(2,1)S(1)} %get-tuple-element.10.strip, bf16[17,16,128,128]{3,2,1,0:T(8,128)(2,1)S(1)} %get-tuple-element.11.panel, ...), custom_call_target="tpu_custom_call" | custom-call | tf_op jit(solution)/shard_map/pallas_call | solution.py:533

commit v8 on v7

--- a/solution.py
+++ b/solution.py
@@ -157,8 +157,8 @@
         def _():
             def step(n, c):
                 lefts, rights = [], []
-                for u in range(4):
-                    k, w = n * 2 + u // 2, u % 2
+                for u in range(8):
+                    k, w = n * 4 + u // 2, u % 2
                     i = p_idx[g, w, k] - low
                     ok = (w < p_idx[g, 2, k]) & (i >= 0) & (i < ROWS)
                     i = jnp.clip(i, 0, ROWS - 1)
@@ -177,7 +177,7 @@
                 acc[...] += 2.0 * product if both else product
                 return c
 
-            lax.fori_loop(0, 4, step, 0)
+            lax.fori_loop(0, 2, step, 0)
 
     def list_pairs():
         def row(i, c):

time: 62.3 us -> 62 us (level)
  no operation moved by 1% of the time
where the time goes in v8:
time: 62 us; the launch traced here: 61.8 us
  Pallas kernels  60 us (97%)
  between operations  1.81 us (3%)
    pallas_call x1, Pallas kernels, on_device(): pl.pallas_call(gather_kernel, out_shape=[pltpu.VMEM((8, OWN, BS, BS), jnp...  57.6 us
    pallas_call x1, Pallas kernels, on_device(): pl.pallas_call(finish_kernel, out_shape=jax.ShapeDtypeStruct((ROWS, YCAP,...  2.39 us

profile of v8, /device:TPU:1, one launch (start us, length us, event | category | flops | bytes accessed | tf_op | source)
XLA Modules:
  0.0 61.8 jit_solution(2577059425250729514)
XLA Ops:
  0.6 57.6 %shard_map.77 = (bf16[8,16,128,128]{3,2,1,0:T(8,128)(2,1)S(1)}, bf16[17,16,128,128]{3,2,1,0:T(8,128)(2,1)S(1)}, bf16[8,12,128,128]{3,2,1,0:T(8,128)(2,1)S(1)}, f...) custom-call(bf16[16,128,128]{2,1,0:T(8,128)(2,1)} %bitcast.8, s32[2,8]{1,0:T(2,128)} %bitcast.9, ...), custom_call_target="tpu_custom_call" | custom-call | tf_op jit(solution)/shard_map/pallas_call | solution.py:489
  58.3 2.4 %shard_map.78 = bf16[8,12,128,128]{3,2,1,0:T(8,128)(2,1)} custom-call(s32[8,128]{1,0:T(8,128)S(1)} %get-tuple-element.8.table, s32[8,128]{1,0:T(8,128)S(1)} %get-tuple-element.9.entries, bf16[8,16,128,128]{3,2,1,0:T(8,128)(2,1)S(1)} %get-tuple-element.10.strip, bf16[17,16,128,128]{3,2,1,0:T(8,128)(2,1)S(1)} %get-tuple-element.11.panel, ...), custom_call_target="tpu_custom_call" | custom-call | tf_op jit(solution)/shard_map/pallas_call | solution.py:533

commit v9 on v8

--- a/solution.py
+++ b/solution.py
@@ -338,14 +338,13 @@
     for q in (0, 1):
         ay[2].arrive(q)
         bz[2].arrive(q)
-    ay[3].own((0,), one)
     bz[3].own()
     list_slots()
     add_chunk(0, 1)
     add_chunk(1, 1)
     bz[0].arrive_across()
     add_chunk(2, 0)
-    ay[3].arrive(1, hold=(1,))
+    ay[3].arrive(1, hold=(0, 1))
     add_chunk(3, 1)
     bz[1].arrive_across()
     add_chunk(2, 1)
@@ -376,7 +375,8 @@
         for n in range(len(far)):
             tell_plane(n).start()
 
-    ay[3].own((0,), two)
+    ay[3].own((0,))
+    ay[3].pass_on(1, 0)
     ay[3].pass_on(1, 1)
 
     for part in (one, two):

time: 62 us -> 61.9 us (level)
  the two profiles are of different devices: /device:TPU:1 before, /device:TPU:0 now
where the time goes in v9:
time: 61.9 us; the launch traced here: 61.3 us
  Pallas kernels  59.5 us (96%)
  between operations  1.81 us (3%)
    pallas_call x1, Pallas kernels, on_device(): pl.pallas_call(gather_kernel, out_shape=[pltpu.VMEM((8, OWN, BS, BS), jnp...  57.1 us
    pallas_call x1, Pallas kernels, on_device(): pl.pallas_call(finish_kernel, out_shape=jax.ShapeDtypeStruct((ROWS, YCAP,...  2.39 us

profile of v9, /device:TPU:0, one launch (start us, length us, event | category | flops | bytes accessed | tf_op | source)
XLA Modules:
  0.0 61.3 jit_solution(2156548479047930368)
XLA Ops:
  0.6 57.1 %shard_map.77 = (bf16[8,16,128,128]{3,2,1,0:T(8,128)(2,1)S(1)}, bf16[17,16,128,128]{3,2,1,0:T(8,128)(2,1)S(1)}, bf16[8,12,128,128]{3,2,1,0:T(8,128)(2,1)S(1)}, f...) custom-call(bf16[16,128,128]{2,1,0:T(8,128)(2,1)} %bitcast.8, s32[2,8]{1,0:T(2,128)} %bitcast.9, ...), custom_call_target="tpu_custom_call" | custom-call | tf_op jit(solution)/shard_map/pallas_call | solution.py:489
  57.8 2.4 %shard_map.78 = bf16[8,12,128,128]{3,2,1,0:T(8,128)(2,1)} custom-call(s32[8,128]{1,0:T(8,128)S(1)} %get-tuple-element.8.table, s32[8,128]{1,0:T(8,128)S(1)} %get-tuple-element.9.entries, bf16[8,16,128,128]{3,2,1,0:T(8,128)(2,1)S(1)} %get-tuple-element.10.strip, bf16[17,16,128,128]{3,2,1,0:T(8,128)(2,1)S(1)} %get-tuple-element.11.panel, ...), custom_call_target="tpu_custom_call" | custom-call | tf_op jit(solution)/shard_map/pallas_call | solution.py:533
